TPU v7x, 512 devices: a whole 4x8x8 slice. The times are simulated.
512 devices in a mesh: gy: 32 (over z, x), gx: 16 (over y, core).
Axes of the slice: x: 4, y: 8, z: 8, core: 2. Of those that a mesh axis runs over, the one named last changes fastest.
Arguments:
- ensemble: float32 [64, 256, 2048], P(None, 'gy', 'gx'), may hold values from -6 to 6
- flow: float32 [3, 256, 2048], P(None, 'gy', 'gx')
- obs_cell: int32 [32, 16, 4], P('gy', 'gx'), may hold values from 0 to 1023
- obs_value: float32 [32, 16, 4], P('gy', 'gx'), may hold values from -6 to 6
- obs_var: float32 [32, 16, 4], P('gy', 'gx'), may hold values from 4 to 16
Outputs:
- analysis: float32 [64, 256, 2048], P(None, 'gy', 'gx')
All inputs are finite; a program needn't handle non-finite values.
Results may differ from a plain program's by a relative error of at most 0.0001.
Values sent between devices are 32-bit elements; how exact they have to be, the bound alone decides.
A program may use at most 64 MiB of HBM per device.

v0:
```python
import jax
import jax.numpy as jnp
from jax import lax
from jax.sharding import PartitionSpec as P


def extended(block, sides, width):
    for axis, dim in sides:
        count = lax.axis_size(axis)
        forward = [(i, i + 1) for i in range(count - 1)]
        backward = [(target, source) for source, target in forward]
        low = lax.ppermute(
            lax.slice_in_dim(block, block.shape[dim] - width, None, axis=dim), axis, forward
        )
        high = lax.ppermute(lax.slice_in_dim(block, 0, width, axis=dim), axis, backward)
        block = jnp.concatenate([low, block, high], axis=dim)
    return block


def advance(padded, coeffs):
    state_grid = padded[:, 1:-1, 1:-1]
    north = padded[:, :-2, 1:-1]
    south = padded[:, 2:, 1:-1]
    west = padded[:, 1:-1, :-2]
    east = padded[:, 1:-1, 2:]
    spread = coeffs[0] * (north + south + west + east - 4.0 * state_grid)
    return state_grid + spread - 0.5 * coeffs[1] * (east - west) - 0.5 * coeffs[2] * (south - north)


def border_update(state_grid, flow):
    padded = extended(state_grid, (("gy", 1), ("gx", 2)), 1)
    return advance(padded, flow)


def tri_solve(matrix, rhs):
    return lax.linalg.triangular_solve(matrix, rhs, left_side=True, lower=True, transpose_a=True)


def body(ensemble, flow, obs_cell, obs_value, obs_var):
    members = ensemble.shape[0]
    predicted_state = border_update(border_update(ensemble, flow), flow)
    ensemble_average = jnp.mean(predicted_state, axis=0)
    member_deviation = predicted_state - ensemble_average
    flat_anomaly = member_deviation.reshape(members, -1)
    cells = obs_cell.reshape(-1)
    factor = lax.rsqrt(obs_var.reshape(-1))
    scaled = jnp.take(flat_anomaly, cells, axis=1) * factor
    innovation = (obs_value.reshape(-1) - jnp.take(ensemble_average.reshape(-1), cells)) * factor
    eye = jnp.eye(members, dtype=jnp.float32)
    local_gram = jnp.dot(scaled, scaled.T, precision=lax.Precision.HIGHEST)
    local_target = jnp.dot(scaled, innovation, precision=lax.Precision.HIGHEST)
    gram, target = lax.psum((local_gram, local_target), ("gy", "gx"))
    lower = jnp.linalg.cholesky(gram + (members - 1.0) * eye)
    inverse = tri_solve(lower, eye)
    weights = jnp.dot(
        inverse,
        jnp.dot(inverse.T, target, precision=lax.Precision.HIGHEST),
        precision=lax.Precision.HIGHEST,
    )
    transform = jnp.sqrt(members - 1.0) * inverse + weights[:, None]
    update = jnp.dot(transform.T, flat_anomaly, precision=lax.Precision.HIGHEST)
    return ensemble_average + update.reshape(member_deviation.shape)


def solution(mesh):
    return jax.shard_map(
        body,
        mesh=mesh,
        in_specs=(
            P(None, "gy", "gx"),
            P(None, "gy", "gx"),
            P("gy", "gx", None),
            P("gy", "gx", None),
            P("gy", "gx", None),
        ),
        out_specs=P(None, "gy", "gx"),
        check_vma=False,
    )
```

profile of v0, /device:TPU:1, one launch (start us, length us, event | category | flops | bytes accessed | tf_op | source)
XLA Modules:
  0.0 169.7 jit_solution(2727058517683121358)
XLA Ops:
  0.0 0.0 copy-start
  0.0 1.1 copy.23
  1.1 0.0 copy-start.1
  1.1 3.9 %collective-permute-start = (f32[64,1,128]{2,0,1:T(8,128)S(1)}, f32[64,1,128]{2,0,1:T(8,128)S(1)}, u32[]{:S(2)}, u32[]{:S(2)}) collective-permute-start(f32[64,1,128]{2,0,1:T(8,128)S(1)} %get-tuple-element.18), channel_id=1, source_target_pairs={{0,16},{16,32},{32,48},{48,64},{64,80},{80,96},{96,112},{112,128},... | collective-permute-start | bytes 98312 | tf_op jit(solution)/shard_map/ppermute | solution.py:12
  5.1 0.0 copy-start.2
  5.1 1.3 collective-permute-start.1
  6.4 0.0 copy-done.1
  6.4 0.0 copy-done.2
  6.4 0.0 collective-permute-done
  6.4 0.0 copy-done
  6.5 3.2 %collective-permute-done.1 = f32[64,1,128]{2,0,1:T(8,128)S(1)} collective-permute-done((f32[64,1,128]{2,0,1:T(8,128)S(1)}, f32[64,1,128]{2,0,1:T(8,128)S(1)}, u32[]{:S(2)}, u32[]{:S(2)}) %collective-permute-start.1) | collective-permute-done | bytes 32800 | tf_op jit(solution)/shard_map/ppermute | solution.py:15
  9.7 0.2 fusion.34
  9.9 5.2 %collective-permute-start.2 = (f32[64,10,1]{2,0,1:T(8,128)S(1)}, f32[64,10,1]{2,0,1:T(8,128)S(1)}, u32[]{:S(2)}, u32[]{:S(2)}) collective-permute-start(f32[64,10,1]{2,0,1:T(8,128)S(1)} %get-tuple-element.11), channel_id=1, source_target_pairs={{0,1},{1,2},{2,3},{3,4},{4,5},{5,6},{6,7},{7,8},{8,9},{9,10},{10,1... | collective-permute-start | bytes 7688 | tf_op jit(solution)/shard_map/ppermute | solution.py:12
  15.1 3.4 %collective-permute-start.3 = (f32[64,10,1]{2,0,1:T(8,128)S(1)}, f32[64,10,1]{2,0,1:T(8,128)S(1)}, u32[]{:S(2)}, u32[]{:S(2)}) collective-permute-start(f32[64,10,1]{2,0,1:T(8,128)S(1)} %get-tuple-element.12), channel_id=1, source_target_pairs={{1,0},{2,1},{3,2},{4,3},{5,4},{6,5},{7,6},{8,7},{9,8},{10,9},{11,1... | collective-permute-start | bytes 7688 | tf_op jit(solution)/shard_map/ppermute | solution.py:15
  18.5 0.6 collective-permute-done.2
  19.1 4.4 %collective-permute-done.3 = f32[64,10,1]{2,0,1:T(8,128)S(1)} collective-permute-done((f32[64,10,1]{2,0,1:T(8,128)S(1)}, f32[64,10,1]{2,0,1:T(8,128)S(1)}, u32[]{:S(2)}, u32[]{:S(2)}) %collective-permute-start.3) | collective-permute-done | bytes 2592 | tf_op jit(solution)/shard_map/ppermute | solution.py:15
  23.5 0.3 multiply_subtract_fusion.1
  23.8 0.0 copy-start.3
  23.8 3.1 %collective-permute-start.4 = (f32[64,1,128]{2,0,1:T(8,128)S(1)}, f32[64,1,128]{2,0,1:T(8,128)S(1)}, u32[]{:S(2)}, u32[]{:S(2)}) collective-permute-start(f32[64,1,128]{2,0,1:T(8,128)S(1)} %get-tuple-element.15), channel_id=1, source_target_pairs={{0,16},{16,32},{32,48},{48,64},{64,80},{80,96},{96,112},{112,128},... | collective-permute-start | bytes 98312 | tf_op jit(solution)/shard_map/ppermute | solution.py:12
  26.9 1.3 collective-permute-start.5
  28.2 0.0 copy-done.3
  28.3 0.0 collective-permute-done.4
  28.3 3.3 %collective-permute-done.5 = f32[64,1,128]{2,0,1:T(8,128)S(1)} collective-permute-done((f32[64,1,128]{2,0,1:T(8,128)S(1)}, f32[64,1,128]{2,0,1:T(8,128)S(1)}, u32[]{:S(2)}, u32[]{:S(2)}) %collective-permute-start.5) | collective-permute-done | bytes 32800 | tf_op jit(solution)/shard_map/ppermute | solution.py:15
  31.6 0.2 fusion.33
  31.8 3.2 %collective-permute-start.6 = (f32[64,10,1]{2,0,1:T(8,128)S(1)}, f32[64,10,1]{2,0,1:T(8,128)S(1)}, u32[]{:S(2)}, u32[]{:S(2)}) collective-permute-start(f32[64,10,1]{2,0,1:T(8,128)S(1)} %get-tuple-element.9), channel_id=1, source_target_pairs={{0,1},{1,2},{2,3},{3,4},{4,5},{5,6},{6,7},{7,8},{8,9},{9,10},{10,1... | collective-permute-start | bytes 7688 | tf_op jit(solution)/shard_map/ppermute | solution.py:12
  35.0 1.9 %collective-permute-start.7 = (f32[64,10,1]{2,0,1:T(8,128)S(1)}, f32[64,10,1]{2,0,1:T(8,128)S(1)}, u32[]{:S(2)}, u32[]{:S(2)}) collective-permute-start(f32[64,10,1]{2,0,1:T(8,128)S(1)} %get-tuple-element.10), channel_id=1, source_target_pairs={{1,0},{2,1},{3,2},{4,3},{5,4},{6,5},{7,6},{8,7},{9,8},{10,9},{11,1... | collective-permute-start | bytes 7688 | tf_op jit(solution)/shard_map/ppermute | solution.py:15
  36.9 2.1 %collective-permute-done.6 = f32[64,10,1]{2,0,1:T(8,128)S(1)} collective-permute-done((f32[64,10,1]{2,0,1:T(8,128)S(1)}, f32[64,10,1]{2,0,1:T(8,128)S(1)}, u32[]{:S(2)}, u32[]{:S(2)}) %collective-permute-start.6) | collective-permute-done | bytes 2592 | tf_op jit(solution)/shard_map/ppermute | solution.py:12
  39.0 4.4 %collective-permute-done.7 = f32[64,10,1]{2,0,1:T(8,128)S(1)} collective-permute-done((f32[64,10,1]{2,0,1:T(8,128)S(1)}, f32[64,10,1]{2,0,1:T(8,128)S(1)}, u32[]{:S(2)}, u32[]{:S(2)}) %collective-permute-start.7) | collective-permute-done | bytes 2592 | tf_op jit(solution)/shard_map/ppermute | solution.py:15
  43.4 0.3 fusion.32
  43.7 0.2 copy.25
  43.9 0.6 gather_fusion
  44.5 0.6 gather_fusion.1
  45.1 0.0 copy-start.4
  45.1 0.3 fusion.13
  45.4 0.3 copy-done.4
  45.8 0.2 convolution_bitcast_fusion.2
  46.0 109.7 %all-reduce = (f32[64,64]{1,0:T(8,128)S(1)}, f32[64]{0:T(128)S(1)}) all-reduce(f32[64,64]{1,0:T(8,128)S(1)} %fusion.13, f32[64]{0:T(128)S(1)} %convolution_bitcast_fusion.2), channel_id=1, replica_groups=mesh['gy'=32,'gx'=16] {'gy','gx'}, use_global_device_ids=true, to_apply=%region_1.2 | all-reduce | flops 4160 | bytes 33280 | tf_op jit(solution)/shard_map/psum | solution.py:52
  155.7 0.1 copy.26
  155.8 5.8 %cholesky.17 = f32[64,64]{1,0:T(8,128)S(1)} custom-call(f32[64,64]{1,0:T(8,128)S(1)} %fusion.7), custom_call_target="Cholesky" | custom-call | tf_op jit(solution)/shard_map/jit(cholesky)/cholesky | solution.py:53
  161.6 0.6 compare_reduce_fusion
  162.3 0.7 fusion.2
  162.9 4.9 %custom-call.6 = f32[1,64,64]{1,2,0:T(8,128)S(1)} custom-call(f32[1,64,64]{2,1,0:T(8,128)S(1)} %fusion.2), custom_call_target="InvertDiagBlocksLowerTriangular" | custom-call | tf_op jit(solution)/shard_map/triangular_solve | solution.py:36
  167.8 0.2 fusion.5
  168.0 0.1 convolution_bitcast_fusion.1
  168.2 0.2 convolution_bitcast_fusion
  168.3 0.5 convolution_add_fusion
  168.8 0.9 copy.29
  (16 shorter events, 0.2 us)
Async XLA Ops:
  0.0 6.4 %copy-start = (f32[64,8,128]{2,1,0:T(8,128)S(1)}, f32[64,8,128]{2,1,0:T(8,128)}, u32[]{:S(2)}) copy-start(f32[64,8,128]{2,1,0:T(8,128)} %param.5) | copy-start | bytes 786436
  1.1 5.3 %copy-start.1 = (f32[3,8,128]{2,1,0:T(8,128)S(1)}, f32[3,8,128]{2,1,0:T(8,128)}, u32[]{:S(2)}) copy-start(f32[3,8,128]{2,1,0:T(8,128)} %param.6) | copy-start | bytes 36868
  1.1 5.3 %collective-permute-start = (f32[64,1,128]{2,0,1:T(8,128)S(1)}, f32[64,1,128]{2,0,1:T(8,128)S(1)}, u32[]{:S(2)}, u32[]{:S(2)}) collective-permute-start(f32[64,1,128]{2,0,1:T(8,128)S(1)} %get-tuple-element.18), channel_id=1, source_target_pairs={{0,16},{16,32},{32,48},{48,64},{64,80},{80,96},{96,112},{112,128},... | collective-permute-start | bytes 98312 | tf_op jit(solution)/shard_map/ppermute | solution.py:12
  5.1 1.3 copy-start.2
  5.1 4.7 %collective-permute-start.1 = (f32[64,1,128]{2,0,1:T(8,128)S(1)}, f32[64,1,128]{2,0,1:T(8,128)S(1)}, u32[]{:S(2)}, u32[]{:S(2)}) collective-permute-start(f32[64,1,128]{2,0,1:T(8,128)S(1)} %get-tuple-element.17), channel_id=1, source_target_pairs={{16,0},{32,16},{48,32},{64,48},{80,64},{96,80},{112,96},{128,112},... | collective-permute-start | bytes 98312 | tf_op jit(solution)/shard_map/ppermute | solution.py:15
  9.9 9.2 %collective-permute-start.2 = (f32[64,10,1]{2,0,1:T(8,128)S(1)}, f32[64,10,1]{2,0,1:T(8,128)S(1)}, u32[]{:S(2)}, u32[]{:S(2)}) collective-permute-start(f32[64,10,1]{2,0,1:T(8,128)S(1)} %get-tuple-element.11), channel_id=1, source_target_pairs={{0,1},{1,2},{2,3},{3,4},{4,5},{5,6},{6,7},{7,8},{8,9},{9,10},{10,1... | collective-permute-start | bytes 7688 | tf_op jit(solution)/shard_map/ppermute | solution.py:12
  15.1 8.4 %collective-permute-start.3 = (f32[64,10,1]{2,0,1:T(8,128)S(1)}, f32[64,10,1]{2,0,1:T(8,128)S(1)}, u32[]{:S(2)}, u32[]{:S(2)}) collective-permute-start(f32[64,10,1]{2,0,1:T(8,128)S(1)} %get-tuple-element.12), channel_id=1, source_target_pairs={{1,0},{2,1},{3,2},{4,3},{5,4},{6,5},{7,6},{8,7},{9,8},{10,9},{11,1... | collective-permute-start | bytes 7688 | tf_op jit(solution)/shard_map/ppermute | solution.py:15
  23.8 4.4 %copy-start.3 = (f32[1,1,4]{2,1,0:T(1,128)S(1)}, f32[1,1,4]{2,1,0:T(1,128)}, u32[]{:S(2)}) copy-start(f32[1,1,4]{2,1,0:T(1,128)} %param.9) | copy-start | bytes 52
  23.8 4.5 %collective-permute-start.4 = (f32[64,1,128]{2,0,1:T(8,128)S(1)}, f32[64,1,128]{2,0,1:T(8,128)S(1)}, u32[]{:S(2)}, u32[]{:S(2)}) collective-permute-start(f32[64,1,128]{2,0,1:T(8,128)S(1)} %get-tuple-element.15), channel_id=1, source_target_pairs={{0,16},{16,32},{32,48},{48,64},{64,80},{80,96},{96,112},{112,128},... | collective-permute-start | bytes 98312 | tf_op jit(solution)/shard_map/ppermute | solution.py:12
  26.9 4.7 %collective-permute-start.5 = (f32[64,1,128]{2,0,1:T(8,128)S(1)}, f32[64,1,128]{2,0,1:T(8,128)S(1)}, u32[]{:S(2)}, u32[]{:S(2)}) collective-permute-start(f32[64,1,128]{2,0,1:T(8,128)S(1)} %get-tuple-element.16), channel_id=1, source_target_pairs={{16,0},{32,16},{48,32},{64,48},{80,64},{96,80},{112,96},{128,112},... | collective-permute-start | bytes 98312 | tf_op jit(solution)/shard_map/ppermute | solution.py:15
  31.8 7.2 %collective-permute-start.6 = (f32[64,10,1]{2,0,1:T(8,128)S(1)}, f32[64,10,1]{2,0,1:T(8,128)S(1)}, u32[]{:S(2)}, u32[]{:S(2)}) collective-permute-start(f32[64,10,1]{2,0,1:T(8,128)S(1)} %get-tuple-element.9), channel_id=1, source_target_pairs={{0,1},{1,2},{2,3},{3,4},{4,5},{5,6},{6,7},{7,8},{8,9},{9,10},{10,1... | collective-permute-start | bytes 7688 | tf_op jit(solution)/shard_map/ppermute | solution.py:12
  35.0 8.4 %collective-permute-start.7 = (f32[64,10,1]{2,0,1:T(8,128)S(1)}, f32[64,10,1]{2,0,1:T(8,128)S(1)}, u32[]{:S(2)}, u32[]{:S(2)}) collective-permute-start(f32[64,10,1]{2,0,1:T(8,128)S(1)} %get-tuple-element.10), channel_id=1, source_target_pairs={{1,0},{2,1},{3,2},{4,3},{5,4},{6,5},{7,6},{8,7},{9,8},{10,9},{11,1... | collective-permute-start | bytes 7688 | tf_op jit(solution)/shard_map/ppermute | solution.py:15
  45.1 0.7 copy-start.4
where the time goes:
time: 170 us
  blocking collectives  110 us (65%)
  starting transfers between devices  23.3 us (14%)
  waiting for transfers between devices  18 us (11%)
  other arithmetic  12.8 us (8%)
  local copies, waits for them, and re-layouts  4.15 us (2%)
    psum x1, blocking collectives, body(): gram, target = lax.psum((local_gram, local_target), ('gy', 'gx'))  110 us
    ppermute x4, starting transfers between devices, extended(): lax.ppermute(lax.slice_in_dim(block, block.shape[dim] - width, None, axis...  15.4 us
    ppermute x4, waiting for transfers between devices, extended(): lax.ppermute(lax.slice_in_dim(block, 0, width, axis=dim), axis, backward)  15.3 us
    ppermute x4, starting transfers between devices, extended(): lax.ppermute(lax.slice_in_dim(block, 0, width, axis=dim), axis, backward)  7.9 us
    another operation x3, other arithmetic, body(): lower = jnp.linalg.cholesky(gram + (members - 1.0) * eye)  6.52 us
    another operation x2, other arithmetic, tri_solve(): lax.linalg.triangular_solve(matrix, rhs, left_side=True, lower=True, tran...  5.55 us
  transfers between devices with their start and end apart: 8, of which 6 were waited for; matrix products, arithmetic and copies ran while one was open for 0% of the time, Pallas kernels for 0%

commit v1 on v0

v1 whole, which is shorter than its diff:
```python
import functools
import math

import jax
import jax.numpy as jnp
from jax import lax
from jax.experimental import pallas as pl
from jax.experimental.pallas import tpu as pltpu
from jax.sharding import PartitionSpec as P

MESH = pl.DeviceIdType.MESH
M = 64
CY = 8
CX = 128
F32 = jnp.float32
BF16 = jnp.bfloat16
NX4 = 4


def iota(shape, dim):
    return lax.broadcasted_iota(jnp.int32, shape, dim)


def step(x, n, s, w, e, k, hu, hv):
    return x + k * (n + s + w + e - 4.0 * x) - hu * (e - w) - hv * (s - n)


def forecast_kernel(
    ngy, ngx,
    x_hbm, flow_hbm, cell_hbm, val_hbm, var_hbm,
    gram_ref, hilo_ref, mean_ref,
    xb, fl, cells, vals, varis, qs, sb, hb, hl, hr, kb, yb, rf, rz, rx,
    load_sem, halo_send, halo_recv, gx_send, gx_recv, z_send, z_recv, x_send, x_recv,
):
    gy = lax.axis_index("gy")
    gx = lax.axis_index("gx")
    nz = ngy // NX4
    up, down = lax.rem(gy + ngy - 1, ngy), lax.rem(gy + 1, ngy)
    left, right = lax.rem(gx + ngx - 1, ngx), lax.rem(gx + 1, ngx)
    zpos = gy // NX4
    xpos = lax.rem(gy, NX4)
    z_partners = [(lax.rem(gy + NX4 * i, ngy), gx) for i in range(1, nz)]
    x_partners = [(zpos * NX4 + lax.rem(xpos + i, NX4), gx) for i in range(1, NX4)]
    gx_partners = [(gy, lax.rem(gx + i, ngx)) for i in range(1, ngx)]
    halo_partners = [
        (up, gx), (down, gx), (gy, left), (gy, right),
        (up, left), (up, right), (down, left), (down, right),
    ]

    loads = [
        pltpu.make_async_copy(x_hbm, xb, load_sem.at[0]),
        pltpu.make_async_copy(flow_hbm, fl, load_sem.at[1]),
        pltpu.make_async_copy(cell_hbm, cells, load_sem.at[2]),
        pltpu.make_async_copy(val_hbm, vals, load_sem.at[3]),
        pltpu.make_async_copy(var_hbm, varis, load_sem.at[4]),
    ]
    for copy in loads:
        copy.start()
    barrier = pltpu.get_barrier_semaphore()
    partners = halo_partners + gx_partners + z_partners + x_partners
    for partner in partners:
        pl.semaphore_signal(barrier, inc=1, device_id=partner, device_id_type=MESH)

    lane = iota((8, CX), 1)
    sub = iota((8, CX), 0)
    edge = (lane <= 1) | (lane >= CX - 2)
    s0, s7 = sub == 0, sub == 7
    l0, l127 = lane == 0, lane == CX - 1

    for copy in loads:
        copy.wait()

    def pack(half):
        def body(i, q):
            for j in range(8):
                m = i * 8 + j
                q = q + pltpu.roll(jnp.where(edge, xb[half * 32 + m], 0.0), 4 * m, 1)
            return q
        return lax.fori_loop(0, 4, body, jnp.zeros((8, CX), F32))

    qa, qb = pack(0), pack(1)
    qs[pl.ds(0, 8), :] = qa
    qs[pl.ds(8, 8), :] = qb
    qc = jnp.where(edge, fl[0], 0.0)
    for i in range(1, 3):
        qc = qc + pltpu.roll(jnp.where(edge, fl[i], 0.0), 4 * i, 1)
    qs[pl.ds(16, 8), :] = qc
    sb[pl.ds(0, M), :] = xb[:, 0, :]
    sb[pl.ds(64, M), :] = xb[:, 1, :]
    sb[pl.ds(136, M), :] = xb[:, 6, :]
    sb[pl.ds(200, M), :] = xb[:, 7, :]
    for i in range(3):
        sb[pl.ds(128 + i, 1), :] = fl[i, 0:1, :]
        sb[pl.ds(131 + i, 1), :] = fl[i, 7:8, :]

    pl.semaphore_wait(barrier, len(partners))

    def remote(src, dst, index, target, send=halo_send, recv=halo_recv):
        return pltpu.make_async_remote_copy(
            src_ref=src, dst_ref=dst, send_sem=send.at[index], recv_sem=recv.at[index],
            device_id=target, device_id_type=MESH,
        )

    halos = [
        remote(sb.at[pl.ds(0, 136), :], hb.at[pl.ds(0, 136), :], 0, (up, gx)),
        remote(sb.at[pl.ds(128, 136), :], hb.at[pl.ds(376, 136), :], 1, (down, gx)),
        remote(qs.at[pl.ds(0, 16), :], kb.at[0], 4, (up, left)),
        remote(qs.at[pl.ds(0, 16), :], kb.at[1], 5, (up, right)),
        remote(qs.at[pl.ds(0, 16), :], kb.at[2], 6, (down, left)),
        remote(qs.at[pl.ds(0, 16), :], kb.at[3], 7, (down, right)),
        remote(qs, hr, 2, (gy, left)),
        remote(qs, hl, 3, (gy, right)),
    ]
    for copy in halos:
        copy.start()
    for copy in halos:
        copy.wait_recv()

    has_up, has_down = gy > 0, gy < ngy - 1
    has_left, has_right = gx > 0, gx < ngx - 1

    def on(flag):
        return jnp.full((8, CX), jnp.where(flag, 1, 0), jnp.int32) > 0

    quad = lane & 3
    west_side = quad >= 2
    hmask = ((sub >= 6) & on(has_up)) | ((sub <= 1) & on(has_down))
    cmask = (west_side & on(has_left)) | ((quad <= 1) & on(has_right))
    kmask = hmask & cmask

    k, hu, hv = fl[0], 0.5 * fl[1], 0.5 * fl[2]

    def flow_rows(i):
        lower = jnp.broadcast_to(hb[pl.ds(128 + i, 1), :], (8, CX))
        upper = jnp.broadcast_to(hb[pl.ds(376 + 3 + i, 1), :], (8, CX))
        return jnp.where(hmask, jnp.where(s7, upper, jnp.where(s0, lower, 0.0)), 0.0)

    def flow_cols(i):
        west = jnp.broadcast_to(hl[pl.ds(16, 8), (4 * i - 1) % CX:(4 * i - 1) % CX + 1], (8, CX))
        east = jnp.broadcast_to(hr[pl.ds(16, 8), 4 * i:4 * i + 1], (8, CX))
        return jnp.where(cmask, jnp.where(west_side, west, east), 0.0)

    kh, uh, vh = flow_rows(0), 0.5 * flow_rows(1), 0.5 * flow_rows(2)
    kc, uc, vc = flow_cols(0), 0.5 * flow_cols(1), 0.5 * flow_cols(2)
    west_cell = quad == 3

    total = jnp.zeros((8, CX), F32)
    for half in range(2):
        q = (qa, qb)[half]
        rows = pl.ds(8 * half, 8)
        ring = jnp.where(cmask, jnp.where(west_side, hl[rows, :], hr[rows, :]), 0.0)
        corner_w = jnp.where(s7, kb[3, rows, :], kb[1, rows, :])
        corner_e = jnp.where(s7, kb[2, rows, :], kb[0, rows, :])
        corner = jnp.where(kmask & (s0 | s7), jnp.where(west_side, corner_w, corner_e), 0.0)
        n = pltpu.roll(jnp.where(s7, corner, ring), 1, 0)
        s = pltpu.roll(jnp.where(s0, corner, ring), 7, 0)
        w = jnp.where(west_cell, pltpu.roll(ring, 1, 1), pltpu.roll(q, 1, 1))
        e = jnp.where(west_cell, pltpu.roll(q, CX - 1, 1), pltpu.roll(ring, CX - 1, 1))
        ring1 = step(ring, n, s, w, e, kc, uc, vc)

        def body(i, acc):
            for j in range(4):
                m = i * 4 + j
                shift = lax.rem(CX - 4 * m, CX)
                member = half * 32 + m
                x = xb[member]
                h = jnp.where(hmask, hb[pl.ds(member, 8, stride=M), :], 0.0)
                ex = pltpu.roll(ring, shift, 1)
                ek = pltpu.roll(corner, shift, 1)
                ey = pltpu.roll(ring1, shift, 1)
                y = step(
                    x,
                    pltpu.roll(jnp.where(s7, h, x), 1, 0), pltpu.roll(jnp.where(s0, h, x), 7, 0),
                    pltpu.roll(jnp.where(l127, ex, x), 1, 1), pltpu.roll(jnp.where(l0, ex, x), CX - 1, 1),
                    k, hu, hv,
                )
                yh = step(
                    h,
                    pltpu.roll(jnp.where(s7, x, h), 1, 0), pltpu.roll(jnp.where(s0, x, h), 7, 0),
                    pltpu.roll(jnp.where(l127, ek, h), 1, 1), pltpu.roll(jnp.where(l0, ek, h), CX - 1, 1),
                    kh, uh, vh,
                )
                z = step(
                    y,
                    pltpu.roll(jnp.where(s7, yh, y), 1, 0), pltpu.roll(jnp.where(s0, yh, y), 7, 0),
                    pltpu.roll(jnp.where(l127, ey, y), 1, 1), pltpu.roll(jnp.where(l0, ey, y), CX - 1, 1),
                    k, hu, hv,
                )
                yb[pl.ds(member * 8, 8), :] = z
                acc = acc + z
            return acc

        total = lax.fori_loop(0, 8, body, total)
    mean = total * (1.0 / M)
    mean_ref[...] = mean

    lane64 = iota((M, CX), 1)
    diag64 = lane64 == iota((M, CX), 0)
    sub4 = iota((4, CX), 0)
    picked, value, variance = [], jnp.zeros((4, CX), F32), jnp.ones((4, CX), F32)
    for j in range(4):
        cell = cells[0, 0, j]
        row, col = lax.shift_right_logical(cell, 7), cell & (CX - 1)
        line = yb[pl.ds(row, M, stride=8), :]
        column = jnp.sum(jnp.where(lane64 == col, line, 0.0), axis=1, keepdims=True)
        picked.append(jnp.sum(jnp.where(diag64, column, 0.0), axis=0, keepdims=True))
        value = jnp.where(sub4 == j, vals[0, 0, j], value)
        variance = jnp.where(sub4 == j, varis[0, 0, j], variance)
    picked = jnp.concatenate(picked, axis=0)
    cell_mean = jnp.sum(picked, axis=1, keepdims=True) * (1.0 / M)
    factor = lax.rsqrt(variance)
    lane4 = iota((4, CX), 1)
    obs = jnp.where(lane4 < M - 1, picked, value)
    obs = jnp.where(lane4 < M, (obs - cell_mean) * factor, 0.0)
    rf[gx] = obs[0:2] + pltpu.roll(obs[2:4], M, 1)

    gx_copies = [
        pltpu.make_async_remote_copy(
            src_ref=rf.at[gx], dst_ref=rf.at[gx], send_sem=gx_send, recv_sem=gx_recv,
            device_id=partner, device_id_type=MESH,
        )
        for partner in gx_partners
    ]
    for copy in gx_copies:
        copy.start()

    for r in range(CY):
        line = yb[pl.ds(r, M, stride=8), :] - mean[r:r + 1, :]
        high = line.astype(BF16)
        hilo_ref[pl.ds(0, M), pl.ds(r * CX, CX)] = high
        hilo_ref[pl.ds(M, M), pl.ds(r * CX, CX)] = (line - high.astype(F32)).astype(BF16)

    def wait_all(buffer, count, sem):
        piece = buffer.at[pl.ds(0, count)]
        pltpu.make_async_copy(piece, piece, sem).wait()

    wait_all(rf, ngx - 1, gx_recv)
    gathered = jnp.concatenate([rf[i] for i in range(ngx)], axis=0)
    lane32 = iota((2 * ngx, CX), 1)
    rows = jnp.concatenate(
        [jnp.where(lane32 < M, gathered, 0.0), jnp.where(lane32 < M, pltpu.roll(gathered, M, 1), 0.0)], axis=0
    )
    gram = jnp.dot(rows.T, rows, precision=lax.Precision.HIGHEST, preferred_element_type=F32)
    rz[zpos] = gram[0:32] + pltpu.roll(gram[32:64], M, 1)

    z_copies = [
        pltpu.make_async_remote_copy(
            src_ref=rz.at[zpos], dst_ref=rz.at[zpos], send_sem=z_send, recv_sem=z_recv,
            device_id=partner, device_id_type=MESH,
        )
        for partner in z_partners
    ]
    for copy in z_copies:
        copy.start()
    wait_all(rz, nz - 1, z_recv)
    part = rz[0]
    for i in range(1, nz):
        part = part + rz[i]
    rx[xpos] = part
    x_copies = [
        pltpu.make_async_remote_copy(
            src_ref=rx.at[xpos], dst_ref=rx.at[xpos], send_sem=x_send, recv_sem=x_recv,
            device_id=partner, device_id_type=MESH,
        )
        for partner in x_partners
    ]
    for copy in x_copies:
        copy.start()
    wait_all(rx, NX4 - 1, x_recv)
    gram_ref[...] = (rx[0] + rx[1]) + (rx[2] + rx[3])

    for copy in halos:
        copy.wait_send()
    wait_all(rf, ngx - 1, gx_send)
    wait_all(rz, nz - 1, z_send)
    wait_all(rx, NX4 - 1, x_send)


def analysis_kernel(gram_ref, hilo_ref, mean_ref, out_ref):
    lane = iota((8, CX), 1)
    sub = iota((8, CX), 0)
    packed = gram_ref[...]
    shifted = pltpu.roll(packed, M, 1)
    blocks = [packed[8 * i:8 * i + 8] for i in range(4)] + [shifted[8 * i:8 * i + 8] for i in range(4)]
    blocks = [jnp.where(lane < M - 1, b, 0.0) for b in blocks]
    row_sums = [jnp.sum(b, axis=1, keepdims=True) for b in blocks]
    last = sub == 7
    target_row = blocks[7][7:8] + jnp.where(lane[0:1] == M - 1, -row_sums[7][7:8], 0.0)
    blocks[7] = jnp.where(last, 0.0, blocks[7])
    row_sums[7] = jnp.where(last[:, 0:1], 0.0, row_sums[7])
    col_sum = functools.reduce(jnp.add, blocks)
    col_sum = jnp.sum(col_sum, axis=0, keepdims=True)
    all_sum = jnp.sum(functools.reduce(jnp.add, row_sums), axis=0, keepdims=True)
    blocks = [jnp.where(lane == M - 1, -r, b) for b, r in zip(blocks, row_sums)]
    blocks[7] = jnp.where(last, jnp.where(lane == M - 1, all_sum, -col_sum), blocks[7])
    eyes = [lane == sub + 8 * i for i in range(8)]
    blocks = [jnp.where(e, b + (M - 1.0), b) for e, b in zip(eyes, blocks)]
    diagonals = [jnp.where(e, b, 0.0) for e, b in zip(eyes, blocks)]
    scale_row = lax.rsqrt(jnp.sum(functools.reduce(jnp.add, diagonals), axis=0, keepdims=True) + jnp.where(lane[0:1] < M, 0.0, 1.0))
    scale_col = [lax.rsqrt(jnp.sum(d, axis=1, keepdims=True)) for d in diagonals]
    a = [
        jnp.where(lane == sub + (M + 8 * i), scale_col[i], jnp.where(lane < M, blocks[i] * scale_col[i] * scale_row, 0.0))
        for i in range(8)
    ]

    lower = [None] * 8
    for p in range(16):
        b, o = p // 2, 4 * (p % 2)
        cols = {
            (t, i): jnp.broadcast_to(a[i][:, 4 * p + t:4 * p + t + 1], (8, CX)) for t in range(4) for i in range(b, 8)
        }
        d = {
            (s, t): jnp.broadcast_to(cols[t, b][o + s:o + s + 1, :], (8, CX)) for s in range(4) for t in range(s + 1)
        }
        r = [jnp.broadcast_to(a[b][o + s:o + s + 1, :], (8, CX)) for s in range(4)]

        det = d[0, 0] * d[1, 1] - d[1, 0] * d[1, 0]
        inv = 1.0 / det
        i00, i10, i11 = d[1, 1] * inv, -d[1, 0] * inv, d[0, 0] * inv
        e00 = i00 * d[2, 0] + i10 * d[2, 1]
        e10 = i10 * d[2, 0] + i11 * d[2, 1]
        e01 = i00 * d[3, 0] + i10 * d[3, 1]
        e11 = i10 * d[3, 0] + i11 * d[3, 1]
        c00 = d[2, 2] - (d[2, 0] * e00 + d[2, 1] * e10)
        c10 = d[3, 2] - (d[3, 0] * e00 + d[3, 1] * e10)
        c11 = d[3, 3] - (d[3, 0] * e01 + d[3, 1] * e11)
        r2 = r[2] - (e00 * r[0] + e10 * r[1])
        r3 = r[3] - (e01 * r[0] + e11 * r[1])
        det2 = c00 * c11 - c10 * c10
        if p < 15:
            u0 = i00 * r[0] + i10 * r[1]
            u1 = i10 * r[0] + i11 * r[1]
            inv2 = 1.0 / det2
            z2 = (c11 * r2 - c10 * r3) * inv2
            z3 = (c00 * r3 - c10 * r2) * inv2
            z0 = u0 - (e00 * z2 + e01 * z3)
            z1 = u1 - (e10 * z2 + e11 * z3)
            z = (z0, z1, z2, z3)
            for i in range(b if o == 0 else b + 1, 8):
                update = (cols[0, i] * z[0] + cols[1, i] * z[1]) + (cols[2, i] * z[2] + cols[3, i] * z[3])
                new = a[i] - update
                a[i] = jnp.where(sub >= 4, new, a[i]) if i == b else new
        n0 = r[0] * lax.rsqrt(d[0, 0])
        n1 = (d[0, 0] * r[1] - d[1, 0] * r[0]) * lax.rsqrt(d[0, 0] * det)
        n2 = r2 * lax.rsqrt(c00)
        n3 = (c00 * r3 - c10 * r2) * lax.rsqrt(c00 * det2)
        rows = jnp.where(sub == o, n0, jnp.where(sub == o + 1, n1, jnp.where(sub == o + 2, n2, n3)))
        lower[b] = rows if o == 0 else jnp.where(sub >= 4, rows, lower[b])
    lower = [pltpu.roll(jnp.where(lane >= M, v, 0.0), M, 1) for v in lower]
    heads = [jnp.sum(v * target_row, axis=1, keepdims=True) for v in lower]
    weight = jnp.sum(functools.reduce(jnp.add, [v * h for v, h in zip(lower, heads)]), axis=0, keepdims=True)
    root = math.sqrt(M - 1.0)
    mix = jnp.concatenate([root * v + weight for v in lower], axis=0)
    high = mix.astype(BF16).astype(F32)
    low = mix - high
    pair = jnp.where(iota((M, CX), 1) < M, high, pltpu.roll(high, M, 1)).astype(BF16)
    low_pair = jnp.where(iota((M, CX), 1) < M, low, pltpu.roll(low, M, 1)).astype(BF16)
    left = jnp.concatenate([pair, low_pair], axis=1)
    for r in range(0, CY, 2):
        cols = pl.ds(r * CX, 2 * CX)
        block = hilo_ref[:, cols]
        right = jnp.concatenate([block, block], axis=0)
        res = jnp.dot(left, right, preferred_element_type=F32)
        out_ref[:, r, :] = res[:, :CX] + mean_ref[r:r + 1, :]
        out_ref[:, r + 1, :] = res[:, CX:] + mean_ref[r + 1:r + 2, :]


def body(ngy, ngx, ensemble, flow, obs_cell, obs_value, obs_var):
    vmem = pl.BlockSpec(memory_space=pltpu.VMEM)
    hbm = pl.BlockSpec(memory_space=pl.ANY)
    dma = pltpu.SemaphoreType.DMA
    gram, hilo, mean = pl.pallas_call(
        functools.partial(forecast_kernel, ngy, ngx),
        out_shape=(
            jax.ShapeDtypeStruct((32, CX), F32),
            jax.ShapeDtypeStruct((2 * M, CY * CX), BF16),
            jax.ShapeDtypeStruct((CY, CX), F32),
        ),
        in_specs=[hbm] * 5,
        out_specs=(vmem,) * 3,
        scratch_shapes=[
            pltpu.VMEM((M, CY, CX), F32),
            pltpu.VMEM((3, CY, CX), F32),
            pltpu.SMEM((1, 1, 4), jnp.int32),
            pltpu.SMEM((1, 1, 4), F32),
            pltpu.SMEM((1, 1, 4), F32),
            pltpu.VMEM((24, CX), F32),
            pltpu.VMEM((264, CX), F32),
            pltpu.VMEM((512, CX), F32),
            pltpu.VMEM((24, CX), F32),
            pltpu.VMEM((24, CX), F32),
            pltpu.VMEM((4, 16, CX), F32),
            pltpu.VMEM((512, CX), F32),
            pltpu.VMEM((ngx, 2, CX), F32),
            pltpu.VMEM((ngy // NX4, 32, CX), F32),
            pltpu.VMEM((NX4, 32, CX), F32),
            dma((5,)), dma((8,)), dma((8,)),
            dma, dma, dma, dma, dma, dma,
        ],
        compiler_params=pltpu.CompilerParams(collective_id=0, has_side_effects=True),
        name="forecast",
    )(ensemble, flow, obs_cell, obs_value, obs_var)
    return pl.pallas_call(
        analysis_kernel,
        out_shape=jax.ShapeDtypeStruct((M, CY, CX), F32),
        in_specs=[vmem] * 3,
        out_specs=vmem,
        name="analysis",
    )(gram, hilo, mean)


def solution(mesh):
    tile = P("gy", "gx", None)
    return jax.shard_map(
        functools.partial(body, mesh.shape["gy"], mesh.shape["gx"]),
        mesh=mesh,
        in_specs=(P(None, "gy", "gx"), P(None, "gy", "gx"), tile, tile, tile),
        out_specs=P(None, "gy", "gx"),
        check_vma=False,
    )
```

time: 170 us -> 44.9 us (0.26)
  the two profiles are of different devices: /device:TPU:1 before, /device:TPU:4 now
where the time goes in v1:
time: 44.9 us; the launch traced here: 44.8 us
  Pallas kernels  44.8 us (100%)
    pallas_call x1, Pallas kernels, body(): pl.pallas_call(functools.partial(forecast_kernel, ngy, ngx), out_shape=(j...  39.6 us
    pallas_call x1, Pallas kernels, body(): pl.pallas_call(analysis_kernel, out_shape=jax.ShapeDtypeStruct((M, CY, CX...  5.18 us

profile of v1, /device:TPU:4, one launch (start us, length us, event | category | flops | bytes accessed | tf_op | source)
XLA Modules:
  0.0 44.8 jit_solution(11023585328953887526)
XLA Ops:
  0.0 39.6 %forecast.1 = (f32[32,128]{1,0:T(8,128)}, bf16[128,1024]{1,0:T(8,128)(2,1)}, f32[8,128]{1,0:T(8,128)}) custom-call(f32[64,8,128]{2,1,0:T(8,128)} %x_hbm.1, f32[3,8,128]{2,1,0:T(8,128)} %flow_hbm.1, s32[1,1,4]{2,1,0:T(1,128)} %cell_hbm.1, f32[1,1,4]{2,1,0:T(1,128)} %val_hbm.1, f32[1,1,4]{2,1,0:T(1,128)} %var_hbm.1), custom_call_target="tpu_custom_call" | custom-call | tf_op jit(solution)/shard_map/forecast/pallas_call | solution.py:372
  39.6 5.2 %analysis.1 = f32[64,8,128]{2,1,0:T(8,128)} custom-call(f32[32,128]{1,0:T(8,128)} %get-tuple-element.8.gram_ref, bf16[128,1024]{1,0:T(8,128)(2,1)} %get-tuple-element.9.hilo_ref, f32[8,128]{1,0:T(8,128)} %get-tuple-element.10.mean_ref), custom_call_target="tpu_custom_call" | custom-call | tf_op jit(solution)/shard_map/analysis/pallas_call | solution.py:403

commit v2 on v1

--- a/solution.py
+++ b/solution.py
@@ -29,23 +29,15 @@
     ngy, ngx,
     x_hbm, flow_hbm, cell_hbm, val_hbm, var_hbm,
     gram_ref, hilo_ref, mean_ref,
-    xb, fl, cells, vals, varis, qs, sb, hb, hl, hr, kb, yb, rf, rz, rx,
-    load_sem, halo_send, halo_recv, gx_send, gx_recv, z_send, z_recv, x_send, x_recv,
+    xb, fl, cells, vals, varis, qs, sb, hb, hl, hr, kb, yb, rf,
+    load_sem, halo_send, halo_recv, gx_send, gx_recv,
 ):
     gy = lax.axis_index("gy")
     gx = lax.axis_index("gx")
-    nz = ngy // NX4
-    up, down = lax.rem(gy + ngy - 1, ngy), lax.rem(gy + 1, ngy)
+    up, down = gy - 1, gy + 1
+    has_up, has_down = gy > 0, gy < ngy - 1
     left, right = lax.rem(gx + ngx - 1, ngx), lax.rem(gx + 1, ngx)
-    zpos = gy // NX4
-    xpos = lax.rem(gy, NX4)
-    z_partners = [(lax.rem(gy + NX4 * i, ngy), gx) for i in range(1, nz)]
-    x_partners = [(zpos * NX4 + lax.rem(xpos + i, NX4), gx) for i in range(1, NX4)]
     gx_partners = [(gy, lax.rem(gx + i, ngx)) for i in range(1, ngx)]
-    halo_partners = [
-        (up, gx), (down, gx), (gy, left), (gy, right),
-        (up, left), (up, right), (down, left), (down, right),
-    ]
 
     loads = [
         pltpu.make_async_copy(x_hbm, xb, load_sem.at[0]),
@@ -57,9 +49,20 @@
     for copy in loads:
         copy.start()
     barrier = pltpu.get_barrier_semaphore()
-    partners = halo_partners + gx_partners + z_partners + x_partners
-    for partner in partners:
-        pl.semaphore_signal(barrier, inc=1, device_id=partner, device_id_type=MESH)
+
+    def greet(partners):
+        for partner in partners:
+            pl.semaphore_signal(barrier, inc=1, device_id=partner, device_id_type=MESH)
+
+    @pl.when(has_up)
+    def _():
+        greet([(up, gx), (up, left), (up, right)])
+
+    @pl.when(has_down)
+    def _():
+        greet([(down, gx), (down, left), (down, right)])
+
+    greet(gx_partners)
 
     lane = iota((8, CX), 1)
     sub = iota((8, CX), 0)
@@ -93,7 +96,14 @@
         sb[pl.ds(128 + i, 1), :] = fl[i, 0:1, :]
         sb[pl.ds(131 + i, 1), :] = fl[i, 7:8, :]
 
-    pl.semaphore_wait(barrier, len(partners))
+    @pl.when(has_up & has_down)
+    def _():
+        pl.semaphore_wait(barrier, ngx + 5)
+
+    @pl.when(jnp.logical_not(has_up & has_down))
+    def _():
+        pl.semaphore_wait(barrier, ngx + 2)
+
 
     def remote(src, dst, index, target, send=halo_send, recv=halo_recv):
         return pltpu.make_async_remote_copy(
@@ -101,22 +111,43 @@
             device_id=target, device_id_type=MESH,
         )
 
-    halos = [
+    up_halos = [
         remote(sb.at[pl.ds(0, 136), :], hb.at[pl.ds(0, 136), :], 0, (up, gx)),
-        remote(sb.at[pl.ds(128, 136), :], hb.at[pl.ds(376, 136), :], 1, (down, gx)),
         remote(qs.at[pl.ds(0, 16), :], kb.at[0], 4, (up, left)),
         remote(qs.at[pl.ds(0, 16), :], kb.at[1], 5, (up, right)),
+    ]
+    down_halos = [
+        remote(sb.at[pl.ds(128, 136), :], hb.at[pl.ds(376, 136), :], 1, (down, gx)),
         remote(qs.at[pl.ds(0, 16), :], kb.at[2], 6, (down, left)),
         remote(qs.at[pl.ds(0, 16), :], kb.at[3], 7, (down, right)),
-        remote(qs, hr, 2, (gy, left)),
-        remote(qs, hl, 3, (gy, right)),
     ]
-    for copy in halos:
+    side_halos = [remote(qs, hr, 2, (gy, left)), remote(qs, hl, 3, (gy, right))]
+
+    @pl.when(has_up)
+    def _():
+        for copy in up_halos:
+            copy.start()
+
+    @pl.when(has_down)
+    def _():
+        for copy in down_halos:
+            copy.start()
+
+    for copy in side_halos:
         copy.start()
-    for copy in halos:
+    for copy in side_halos:
         copy.wait_recv()
 
-    has_up, has_down = gy > 0, gy < ngy - 1
+    @pl.when(has_up)
+    def _():
+        for copy in down_halos:
+            copy.wait_recv()
+
+    @pl.when(has_down)
+    def _():
+        for copy in up_halos:
+            copy.wait_recv()
+
     has_left, has_right = gx > 0, gx < ngx - 1
 
     def on(flag):
@@ -230,10 +261,6 @@
         hilo_ref[pl.ds(0, M), pl.ds(r * CX, CX)] = high
         hilo_ref[pl.ds(M, M), pl.ds(r * CX, CX)] = (line - high.astype(F32)).astype(BF16)
 
-    def wait_all(buffer, count, sem):
-        piece = buffer.at[pl.ds(0, count)]
-        pltpu.make_async_copy(piece, piece, sem).wait()
-
     wait_all(rf, ngx - 1, gx_recv)
     gathered = jnp.concatenate([rf[i] for i in range(ngx)], axis=0)
     lane32 = iota((2 * ngx, CX), 1)
@@ -241,37 +268,59 @@
         [jnp.where(lane32 < M, gathered, 0.0), jnp.where(lane32 < M, pltpu.roll(gathered, M, 1), 0.0)], axis=0
     )
     gram = jnp.dot(rows.T, rows, precision=lax.Precision.HIGHEST, preferred_element_type=F32)
-    rz[zpos] = gram[0:32] + pltpu.roll(gram[32:64], M, 1)
-
-    z_copies = [
-        pltpu.make_async_remote_copy(
-            src_ref=rz.at[zpos], dst_ref=rz.at[zpos], send_sem=z_send, recv_sem=z_recv,
-            device_id=partner, device_id_type=MESH,
-        )
-        for partner in z_partners
-    ]
-    for copy in z_copies:
-        copy.start()
+    gram_ref[...] = gram[0:32] + pltpu.roll(gram[32:64], M, 1)
+
+    for copy in side_halos:
+        copy.wait_send()
+
+    @pl.when(has_up)
+    def _():
+        for copy in up_halos:
+            copy.wait_send()
+
+    @pl.when(has_down)
+    def _():
+        for copy in down_halos:
+            copy.wait_send()
+
+    wait_all(rf, ngx - 1, gx_send)
+
+
+def wait_all(buffer, count, sem):
+    piece = buffer.at[pl.ds(0, count)]
+    pltpu.make_async_copy(piece, piece, sem).wait()
+
+
+def sum_kernel(ngy, part_ref, gram_ref, rz, rx, z_send, z_recv, x_send, x_recv):
+    gy = lax.axis_index("gy")
+    gx = lax.axis_index("gx")
+    nz = ngy // NX4
+    zpos = gy // NX4
+    xpos = lax.rem(gy, NX4)
+    z_partners = [(lax.rem(gy + NX4 * i, ngy), gx) for i in range(1, nz)]
+    x_partners = [(zpos * NX4 + lax.rem(xpos + i, NX4), gx) for i in range(1, NX4)]
+    barrier = pltpu.get_barrier_semaphore()
+    for partner in z_partners + x_partners:
+        pl.semaphore_signal(barrier, inc=1, device_id=partner, device_id_type=MESH)
+    rz[zpos] = part_ref[...]
+    pl.semaphore_wait(barrier, nz + NX4 - 2)
+
+    def spread(buffer, slot, partners, send, recv):
+        for partner in partners:
+            pltpu.make_async_remote_copy(
+                src_ref=buffer.at[slot], dst_ref=buffer.at[slot], send_sem=send, recv_sem=recv,
+                device_id=partner, device_id_type=MESH,
+            ).start()
+
+    spread(rz, zpos, z_partners, z_send, z_recv)
     wait_all(rz, nz - 1, z_recv)
     part = rz[0]
     for i in range(1, nz):
         part = part + rz[i]
     rx[xpos] = part
-    x_copies = [
-        pltpu.make_async_remote_copy(
-            src_ref=rx.at[xpos], dst_ref=rx.at[xpos], send_sem=x_send, recv_sem=x_recv,
-            device_id=partner, device_id_type=MESH,
-        )
-        for partner in x_partners
-    ]
-    for copy in x_copies:
-        copy.start()
+    spread(rx, xpos, x_partners, x_send, x_recv)
     wait_all(rx, NX4 - 1, x_recv)
     gram_ref[...] = (rx[0] + rx[1]) + (rx[2] + rx[3])
-
-    for copy in halos:
-        copy.wait_send()
-    wait_all(rf, ngx - 1, gx_send)
     wait_all(rz, nz - 1, z_send)
     wait_all(rx, NX4 - 1, x_send)
 
@@ -365,16 +414,20 @@
         out_ref[:, r + 1, :] = res[:, CX:] + mean_ref[r + 1:r + 2, :]
 
 
+def near(array):
+    return pltpu.with_memory_space_constraint(array, pltpu.VMEM)
+
+
 def body(ngy, ngx, ensemble, flow, obs_cell, obs_value, obs_var):
     vmem = pl.BlockSpec(memory_space=pltpu.VMEM)
     hbm = pl.BlockSpec(memory_space=pl.ANY)
     dma = pltpu.SemaphoreType.DMA
-    gram, hilo, mean = pl.pallas_call(
+    part, hilo, mean = pl.pallas_call(
         functools.partial(forecast_kernel, ngy, ngx),
         out_shape=(
-            jax.ShapeDtypeStruct((32, CX), F32),
-            jax.ShapeDtypeStruct((2 * M, CY * CX), BF16),
-            jax.ShapeDtypeStruct((CY, CX), F32),
+            pltpu.VMEM((32, CX), F32),
+            pltpu.VMEM((2 * M, CY * CX), BF16),
+            pltpu.VMEM((CY, CX), F32),
         ),
         in_specs=[hbm] * 5,
         out_specs=(vmem,) * 3,
@@ -392,21 +445,31 @@
             pltpu.VMEM((4, 16, CX), F32),
             pltpu.VMEM((512, CX), F32),
             pltpu.VMEM((ngx, 2, CX), F32),
-            pltpu.VMEM((ngy // NX4, 32, CX), F32),
-            pltpu.VMEM((NX4, 32, CX), F32),
-            dma((5,)), dma((8,)), dma((8,)),
-            dma, dma, dma, dma, dma, dma,
+            dma((5,)), dma((8,)), dma((8,)), dma, dma,
         ],
         compiler_params=pltpu.CompilerParams(collective_id=0, has_side_effects=True),
         name="forecast",
     )(ensemble, flow, obs_cell, obs_value, obs_var)
+    gram = pl.pallas_call(
+        functools.partial(sum_kernel, ngy),
+        out_shape=pltpu.VMEM((32, CX), F32),
+        in_specs=[vmem],
+        out_specs=vmem,
+        scratch_shapes=[
+            pltpu.VMEM((ngy // NX4, 32, CX), F32),
+            pltpu.VMEM((NX4, 32, CX), F32),
+            dma, dma, dma, dma,
+        ],
+        compiler_params=pltpu.CompilerParams(collective_id=1, has_side_effects=True),
+        name="sums",
+    )(near(part))
     return pl.pallas_call(
         analysis_kernel,
         out_shape=jax.ShapeDtypeStruct((M, CY, CX), F32),
         in_specs=[vmem] * 3,
         out_specs=vmem,
         name="analysis",
-    )(gram, hilo, mean)
+    )(near(gram), near(hilo), near(mean))
 
 
 def solution(mesh):

time: 44.9 us -> 44.4 us (0.989)
  the two profiles are of different devices: /device:TPU:4 before, /device:TPU:1 now
where the time goes in v2:
time: 44.4 us; the launch traced here: 44.3 us
  Pallas kernels  44.3 us (100%)
    pallas_call x1, Pallas kernels, body(): pl.pallas_call(functools.partial(forecast_kernel, ngy, ngx), out_shape=(p...  21.3 us
    pallas_call x1, Pallas kernels, body(): pl.pallas_call(functools.partial(sum_kernel, ngy), out_shape=pltpu.VMEM((...  18.7 us
    pallas_call x1, Pallas kernels, body(): pl.pallas_call(analysis_kernel, out_shape=jax.ShapeDtypeStruct((M, CY, CX...  4.23 us

profile of v2, /device:TPU:1, one launch (start us, length us, event | category | flops | bytes accessed | tf_op | source)
XLA Modules:
  0.0 44.3 jit_solution(13661255165250500190)
XLA Ops:
  0.0 21.3 %forecast.1 = (f32[32,128]{1,0:T(8,128)S(1)}, bf16[128,1024]{1,0:T(8,128)(2,1)S(1)}, f32[8,128]{1,0:T(8,128)S(1)}) custom-call(f32[64,8,128]{2,1,0:T(8,128)} %x_hbm.1, f32[3,8,128]{2,1,0:T(8,128)} %flow_hbm.1, s32[1,1,4]{2,1,0:T(1,128)} %cell_hbm.1, f32[1,1,4]{2,1,0:T(1,128)} %val_hbm.1, f32[1,1,4]{2,1,0:T(1,128)} %var_hbm.1), custom_call_target="tpu_custom_call" | custom-call | tf_op jit(solution)/shard_map/forecast/pallas_call | solution.py:425
  21.3 18.7 %sums.1.gram_ref = f32[32,128]{1,0:T(8,128)S(1)} custom-call(f32[32,128]{1,0:T(8,128)S(1)} %get-tuple-element.8.part_ref), custom_call_target="tpu_custom_call" | custom-call | tf_op jit(solution)/shard_map/sums/pallas_call | solution.py:453
  40.0 4.2 %analysis.1 = f32[64,8,128]{2,1,0:T(8,128)} custom-call(f32[32,128]{1,0:T(8,128)S(1)} %sums.1.gram_ref, bf16[128,1024]{1,0:T(8,128)(2,1)S(1)} %get-tuple-element.9.hilo_ref, f32[8,128]{1,0:T(8,128)S(1)} %get-tuple-element.10.mean_ref), custom_call_target="tpu_custom_call" | custom-call | tf_op jit(solution)/shard_map/analysis/pallas_call | solution.py:466

commit v3 on v2

--- a/solution.py
+++ b/solution.py
@@ -29,8 +29,8 @@
     ngy, ngx,
     x_hbm, flow_hbm, cell_hbm, val_hbm, var_hbm,
     gram_ref, hilo_ref, mean_ref,
-    xb, fl, cells, vals, varis, qs, sb, hb, hl, hr, kb, yb, rf,
-    load_sem, halo_send, halo_recv, gx_send, gx_recv,
+    xb, xr, yr, zr, fl, cf, cells, vals, varis, qs, fs, hu_rows, hd_rows, hl, hr, kb, fh, zc, rf,
+    load_sem, halo_send, halo_recv, flow_send, flow_recv, gx_send, gx_recv,
 ):
     gy = lax.axis_index("gy")
     gx = lax.axis_index("gx")
@@ -39,14 +39,16 @@
     left, right = lax.rem(gx + ngx - 1, ngx), lax.rem(gx + 1, ngx)
     gx_partners = [(gy, lax.rem(gx + i, ngx)) for i in range(1, ngx)]
 
+    row_loads = [pltpu.make_async_copy(x_hbm.at[:, r, :], xr.at[r + 1], load_sem.at[5 + r]) for r in (0, 1, 6, 7, 2, 3, 4, 5)]
+    flow_load = pltpu.make_async_copy(flow_hbm, fl, load_sem.at[1])
     loads = [
         pltpu.make_async_copy(x_hbm, xb, load_sem.at[0]),
-        pltpu.make_async_copy(flow_hbm, fl, load_sem.at[1]),
         pltpu.make_async_copy(cell_hbm, cells, load_sem.at[2]),
         pltpu.make_async_copy(val_hbm, vals, load_sem.at[3]),
         pltpu.make_async_copy(var_hbm, varis, load_sem.at[4]),
     ]
-    for copy in loads:
+    flow_load.start()
+    for copy in row_loads + loads:
         copy.start()
     barrier = pltpu.get_barrier_semaphore()
 
@@ -69,41 +71,9 @@
     edge = (lane <= 1) | (lane >= CX - 2)
     s0, s7 = sub == 0, sub == 7
     l0, l127 = lane == 0, lane == CX - 1
-
-    for copy in loads:
-        copy.wait()
-
-    def pack(half):
-        def body(i, q):
-            for j in range(8):
-                m = i * 8 + j
-                q = q + pltpu.roll(jnp.where(edge, xb[half * 32 + m], 0.0), 4 * m, 1)
-            return q
-        return lax.fori_loop(0, 4, body, jnp.zeros((8, CX), F32))
-
-    qa, qb = pack(0), pack(1)
-    qs[pl.ds(0, 8), :] = qa
-    qs[pl.ds(8, 8), :] = qb
-    qc = jnp.where(edge, fl[0], 0.0)
-    for i in range(1, 3):
-        qc = qc + pltpu.roll(jnp.where(edge, fl[i], 0.0), 4 * i, 1)
-    qs[pl.ds(16, 8), :] = qc
-    sb[pl.ds(0, M), :] = xb[:, 0, :]
-    sb[pl.ds(64, M), :] = xb[:, 1, :]
-    sb[pl.ds(136, M), :] = xb[:, 6, :]
-    sb[pl.ds(200, M), :] = xb[:, 7, :]
-    for i in range(3):
-        sb[pl.ds(128 + i, 1), :] = fl[i, 0:1, :]
-        sb[pl.ds(131 + i, 1), :] = fl[i, 7:8, :]
-
-    @pl.when(has_up & has_down)
-    def _():
-        pl.semaphore_wait(barrier, ngx + 5)
-
-    @pl.when(jnp.logical_not(has_up & has_down))
-    def _():
-        pl.semaphore_wait(barrier, ngx + 2)
-
+    quad = lane & 3
+    q0, q1, q3 = quad == 0, quad == 1, quad == 3
+    west_side = quad >= 2
 
     def remote(src, dst, index, target, send=halo_send, recv=halo_recv):
         return pltpu.make_async_remote_copy(
@@ -111,139 +81,245 @@
             device_id=target, device_id_type=MESH,
         )
 
-    up_halos = [
-        remote(sb.at[pl.ds(0, 136), :], hb.at[pl.ds(0, 136), :], 0, (up, gx)),
-        remote(qs.at[pl.ds(0, 16), :], kb.at[0], 4, (up, left)),
-        remote(qs.at[pl.ds(0, 16), :], kb.at[1], 5, (up, right)),
+    up_flow = [remote(fs.at[0], fh.at[0], 0, (up, gx), flow_send, flow_recv)]
+    down_flow = [remote(fs.at[0], fh.at[1], 1, (down, gx), flow_send, flow_recv)]
+    side_flow = [
+        remote(fs.at[1], fh.at[2], 2, (gy, left), flow_send, flow_recv),
+        remote(fs.at[1], fh.at[3], 3, (gy, right), flow_send, flow_recv),
     ]
-    down_halos = [
-        remote(sb.at[pl.ds(128, 136), :], hb.at[pl.ds(376, 136), :], 1, (down, gx)),
-        remote(qs.at[pl.ds(0, 16), :], kb.at[2], 6, (down, left)),
-        remote(qs.at[pl.ds(0, 16), :], kb.at[3], 7, (down, right)),
-    ]
+    up_rows = [remote(xr.at[pl.ds(1, 2)], hd_rows, 0, (up, gx))]
+    down_rows = [remote(xr.at[pl.ds(7, 2)], hu_rows, 1, (down, gx))]
+    up_corners = [remote(qs, kb.at[0], 4, (up, left)), remote(qs, kb.at[1], 5, (up, right))]
+    down_corners = [remote(qs, kb.at[2], 6, (down, left)), remote(qs, kb.at[3], 7, (down, right))]
     side_halos = [remote(qs, hr, 2, (gy, left)), remote(qs, hl, 3, (gy, right))]
 
-    @pl.when(has_up)
+    def start(up_copies, down_copies, side_copies=()):
+        @pl.when(has_up)
+        def _():
+            for copy in up_copies:
+                copy.start()
+
+        @pl.when(has_down)
+        def _():
+            for copy in down_copies:
+                copy.start()
+
+        for copy in side_copies:
+            copy.start()
+
+    def received(up_copies, down_copies, side_copies=()):
+        for copy in side_copies:
+            copy.wait_recv()
+
+        @pl.when(has_up)
+        def _():
+            for copy in down_copies:
+                copy.wait_recv()
+
+        @pl.when(has_down)
+        def _():
+            for copy in up_copies:
+                copy.wait_recv()
+
+    def sent(up_copies, down_copies, side_copies=()):
+        for copy in side_copies:
+            copy.wait_send()
+
+        @pl.when(has_up)
+        def _():
+            for copy in up_copies:
+                copy.wait_send()
+
+        @pl.when(has_down)
+        def _():
+            for copy in down_copies:
+                copy.wait_send()
+
+    flow_load.wait()
+    qc = jnp.where(edge, fl[0], 0.0)
+    for i in range(1, 3):
+        qc = qc + pltpu.roll(jnp.where(edge, fl[i], 0.0), 4 * i, 1)
+    fs[1] = qc
+    for i in range(3):
+        fs[0, pl.ds(i, 1), :] = fl[i, 0:1, :]
+        fs[0, pl.ds(3 + i, 1), :] = fl[i, 7:8, :]
+    for copy in row_loads[:4]:
+        copy.wait()
+
+    @pl.when(has_up & has_down)
     def _():
-        for copy in up_halos:
-            copy.start()
-
-    @pl.when(has_down)
+        pl.semaphore_wait(barrier, ngx + 5)
+
+    @pl.when(jnp.logical_not(has_up & has_down))
     def _():
-        for copy in down_halos:
-            copy.start()
-
-    for copy in side_halos:
-        copy.start()
-    for copy in side_halos:
-        copy.wait_recv()
-
-    @pl.when(has_up)
-    def _():
-        for copy in down_halos:
-            copy.wait_recv()
-
-    @pl.when(has_down)
-    def _():
-        for copy in up_halos:
-            copy.wait_recv()
+        pl.semaphore_wait(barrier, ngx + 2)
+
+    start(up_rows, down_rows)
+    start(up_flow, down_flow, side_flow)
+    for copy in row_loads[4:] + loads:
+        copy.wait()
+
+    def pack(half):
+        def body(i, q):
+            for j in range(8):
+                m = i * 8 + j
+                q = q + pltpu.roll(jnp.where(edge, xb[half * 32 + m], 0.0), lax.rem(CX - 4 * m, CX), 1)
+            return q
+        return lax.fori_loop(0, 4, body, jnp.zeros((8, CX), F32))
+
+    qa, qb = pack(0), pack(1)
+    qs[pl.ds(0, 8), :] = qa
+    qs[pl.ds(8, 8), :] = qb
+    start(up_corners, down_corners, side_halos)
+
+    def weights(f0, f1, f2):
+        hu, hv = 0.5 * f1, 0.5 * f2
+        return 1.0 - 4.0 * f0, f0 + hv, f0 - hv, f0 + hu, f0 - hu
+
+    own = weights(fl[0], fl[1], fl[2])
+    a0, an, as_, aw, ae = own
+    aw_in, ae_in = jnp.where(l0, 0.0, aw), jnp.where(l127, 0.0, ae)
+    for i, v in enumerate((a0, an, as_, aw_in, ae_in)):
+        cf[i] = v
+
+    blank = jnp.zeros((M, CX), F32)
+    xr[0] = blank
+    xr[9] = blank
+    yr[0] = blank
+    yr[9] = blank
+
+    def inner(source, target, shift):
+        def body(r, carry):
+            c = [jnp.broadcast_to(cf[i, pl.ds(r, 1), :], (8, CX)) for i in range(5)]
+            for b in range(8):
+                rows = pl.ds(8 * b, 8)
+                x = source[r + 1, rows, :]
+                target[r + shift, rows, :] = (
+                    (c[0] * x + c[1] * source[r, rows, :]) + (c[2] * source[r + 2, rows, :] + c[3] * pltpu.roll(x, 1, 1))
+                    + c[4] * pltpu.roll(x, CX - 1, 1)
+                )
+            return carry
+        lax.fori_loop(0, CY, body, 0)
+
+    inner(xr, yr, 1)
+    inner(yr, zr, 0)
+
+    def col(v, l):
+        return jnp.broadcast_to(v[:, l:l + 1], (8, CX))
+
+    c_edge = jnp.where(q0, col(aw, 0), jnp.where(q3, col(ae, CX - 1), 0.0))
+    a0_edge = jnp.where(q0, col(a0, 0), col(a0, CX - 1))
+    an_edge = jnp.where(s0, 0.0, jnp.where(q0, col(an, 0), col(an, CX - 1)))
+    as_edge = jnp.where(s7, 0.0, jnp.where(q0, col(as_, 0), col(as_, CX - 1)))
+    c_next = jnp.where(q1, col(aw, 1), col(ae, CX - 2))
 
     has_left, has_right = gx > 0, gx < ngx - 1
 
     def on(flag):
         return jnp.full((8, CX), jnp.where(flag, 1, 0), jnp.int32) > 0
 
-    quad = lane & 3
-    west_side = quad >= 2
-    hmask = ((sub >= 6) & on(has_up)) | ((sub <= 1) & on(has_down))
+    hmask = (s7 & on(has_up)) | (s0 & on(has_down))
     cmask = (west_side & on(has_left)) | ((quad <= 1) & on(has_right))
-    kmask = hmask & cmask
-
-    k, hu, hv = fl[0], 0.5 * fl[1], 0.5 * fl[2]
-
-    def flow_rows(i):
-        lower = jnp.broadcast_to(hb[pl.ds(128 + i, 1), :], (8, CX))
-        upper = jnp.broadcast_to(hb[pl.ds(376 + 3 + i, 1), :], (8, CX))
-        return jnp.where(hmask, jnp.where(s7, upper, jnp.where(s0, lower, 0.0)), 0.0)
+
+    received(up_flow, down_flow, side_flow)
 
     def flow_cols(i):
-        west = jnp.broadcast_to(hl[pl.ds(16, 8), (4 * i - 1) % CX:(4 * i - 1) % CX + 1], (8, CX))
-        east = jnp.broadcast_to(hr[pl.ds(16, 8), 4 * i:4 * i + 1], (8, CX))
+        west, east = col(fh[3], (4 * i - 1) % CX), col(fh[2], 4 * i)
         return jnp.where(cmask, jnp.where(west_side, west, east), 0.0)
 
-    kh, uh, vh = flow_rows(0), 0.5 * flow_rows(1), 0.5 * flow_rows(2)
     kc, uc, vc = flow_cols(0), 0.5 * flow_cols(1), 0.5 * flow_cols(2)
-    west_cell = quad == 3
-
-    total = jnp.zeros((8, CX), F32)
+
+    def outer_row(tile, offset, flag):
+        fields = [jnp.where(on(flag), jnp.broadcast_to(tile[offset + i:offset + i + 1, :], (8, CX)), 0.0) for i in range(3)]
+        return weights(*fields)
+
+    def line(v, r):
+        return jnp.broadcast_to(v[r:r + 1, :], (8, CX))
+
+    def outside(above):
+        if above:
+            t0, tn, ts, tw, te = outer_row(fh[1], 3, has_up)
+            r, near, far, cross, toward = 0, line(an, 0), tn, ts, line(an, 1)
+        else:
+            t0, tn, ts, tw, te = outer_row(fh[0], 0, has_down)
+            r, near, far, cross, toward = 7, line(as_, 7), ts, tn, line(as_, 6)
+        west = near * jnp.where(l0, 0.0, tw) + line(aw_in, r) * pltpu.roll(near, 1, 1)
+        east = near * jnp.where(l127, 0.0, te) + line(ae_in, r) * pltpu.roll(near, CX - 1, 1)
+        corner = jnp.where(q0, col(near * tw, 0), jnp.where(q3, col(near * te, CX - 1), 0.0))
+        return (near * (t0 + line(a0, r)), near * far, near * cross, west, east, toward * near), corner
+
+    above, corner_above = outside(True)
+    below, corner_below = outside(False)
+    c_corner = jnp.where(s0, corner_above, jnp.where(s7, corner_below, 0.0))
+
+    received(up_corners, down_corners, side_halos)
+    west_cell = q3
     for half in range(2):
         q = (qa, qb)[half]
         rows = pl.ds(8 * half, 8)
         ring = jnp.where(cmask, jnp.where(west_side, hl[rows, :], hr[rows, :]), 0.0)
         corner_w = jnp.where(s7, kb[3, rows, :], kb[1, rows, :])
         corner_e = jnp.where(s7, kb[2, rows, :], kb[0, rows, :])
-        corner = jnp.where(kmask & (s0 | s7), jnp.where(west_side, corner_w, corner_e), 0.0)
+        corner = jnp.where(hmask & cmask, jnp.where(west_side, corner_w, corner_e), 0.0)
         n = pltpu.roll(jnp.where(s7, corner, ring), 1, 0)
         s = pltpu.roll(jnp.where(s0, corner, ring), 7, 0)
-        w = jnp.where(west_cell, pltpu.roll(ring, 1, 1), pltpu.roll(q, 1, 1))
-        e = jnp.where(west_cell, pltpu.roll(q, CX - 1, 1), pltpu.roll(ring, CX - 1, 1))
+        ring_w, ring_e = pltpu.roll(ring, 1, 1), pltpu.roll(ring, CX - 1, 1)
+        w = jnp.where(west_cell, ring_w, pltpu.roll(q, 1, 1))
+        e = jnp.where(west_cell, pltpu.roll(q, CX - 1, 1), ring_e)
         ring1 = step(ring, n, s, w, e, kc, uc, vc)
-
-        def body(i, acc):
-            for j in range(4):
-                m = i * 4 + j
-                shift = lax.rem(CX - 4 * m, CX)
-                member = half * 32 + m
-                x = xb[member]
-                h = jnp.where(hmask, hb[pl.ds(member, 8, stride=M), :], 0.0)
-                ex = pltpu.roll(ring, shift, 1)
-                ek = pltpu.roll(corner, shift, 1)
-                ey = pltpu.roll(ring1, shift, 1)
-                y = step(
-                    x,
-                    pltpu.roll(jnp.where(s7, h, x), 1, 0), pltpu.roll(jnp.where(s0, h, x), 7, 0),
-                    pltpu.roll(jnp.where(l127, ex, x), 1, 1), pltpu.roll(jnp.where(l0, ex, x), CX - 1, 1),
-                    k, hu, hv,
+        x1 = jnp.where(q0, ring_w, ring_e)
+        y1 = jnp.where(q0, pltpu.roll(ring1, 1, 1), pltpu.roll(ring1, CX - 1, 1))
+        outer = jnp.where(s0, pltpu.roll(corner, 1, 0), pltpu.roll(corner, 7, 0))
+        outer = jnp.where(q0, pltpu.roll(outer, 1, 1), pltpu.roll(outer, CX - 1, 1))
+        d = c_edge * x1
+        at_edge = a0_edge * d + an_edge * pltpu.roll(d, 1, 0) + as_edge * pltpu.roll(d, 7, 0) + c_edge * y1 + c_corner * outer
+        inside = c_next * jnp.where(q1, pltpu.roll(d, 1, 1), pltpu.roll(d, CX - 1, 1))
+        zc[half] = jnp.where(q0 | q3, at_edge, inside)
+
+    received(up_rows, down_rows)
+
+    def add_rows(flag, c, near_row, far_row, r, r_in):
+        @pl.when(flag)
+        def _():
+            for b in range(8):
+                rows = pl.ds(8 * b, 8)
+                p = near_row[rows, :]
+                zr[r, rows, :] = zr[r, rows, :] + (
+                    (c[0] * p + c[1] * far_row[rows, :]) + (c[2] * xr[r + 1, rows, :] + c[3] * pltpu.roll(p, 1, 1))
+                    + c[4] * pltpu.roll(p, CX - 1, 1)
                 )
-                yh = step(
-                    h,
-                    pltpu.roll(jnp.where(s7, x, h), 1, 0), pltpu.roll(jnp.where(s0, x, h), 7, 0),
-                    pltpu.roll(jnp.where(l127, ek, h), 1, 1), pltpu.roll(jnp.where(l0, ek, h), CX - 1, 1),
-                    kh, uh, vh,
-                )
-                z = step(
-                    y,
-                    pltpu.roll(jnp.where(s7, yh, y), 1, 0), pltpu.roll(jnp.where(s0, yh, y), 7, 0),
-                    pltpu.roll(jnp.where(l127, ey, y), 1, 1), pltpu.roll(jnp.where(l0, ey, y), CX - 1, 1),
-                    k, hu, hv,
-                )
-                yb[pl.ds(member * 8, 8), :] = z
-                acc = acc + z
-            return acc
-
-        total = lax.fori_loop(0, 8, body, total)
-    mean = total * (1.0 / M)
-    mean_ref[...] = mean
+                zr[r_in, rows, :] = zr[r_in, rows, :] + c[5] * p
+
+    add_rows(has_up, above, hu_rows.at[1], hu_rows.at[0], 0, 1)
+    add_rows(has_down, below, hd_rows.at[0], hd_rows.at[1], 7, 6)
+
+    def add_columns(r, carry):
+        lines = [jnp.broadcast_to(zc[half, pl.ds(r, 1), :], (8, CX)) for half in range(2)]
+        for b in range(8):
+            rows = pl.ds(8 * b, 8)
+            spread = pltpu.roll(lines[b // 4], 32 * (b % 4), 1, stride=4, stride_axis=0)
+            zr[r, rows, :] = zr[r, rows, :] + jnp.where(edge, spread, 0.0)
+        return carry
+
+    lax.fori_loop(0, CY, add_columns, 0)
 
     lane64 = iota((M, CX), 1)
     diag64 = lane64 == iota((M, CX), 0)
-    sub4 = iota((4, CX), 0)
-    picked, value, variance = [], jnp.zeros((4, CX), F32), jnp.ones((4, CX), F32)
+    ones = jnp.zeros((1, CX), F32)
+    picked = []
     for j in range(4):
         cell = cells[0, 0, j]
-        row, col = lax.shift_right_logical(cell, 7), cell & (CX - 1)
-        line = yb[pl.ds(row, M, stride=8), :]
-        column = jnp.sum(jnp.where(lane64 == col, line, 0.0), axis=1, keepdims=True)
-        picked.append(jnp.sum(jnp.where(diag64, column, 0.0), axis=0, keepdims=True))
-        value = jnp.where(sub4 == j, vals[0, 0, j], value)
-        variance = jnp.where(sub4 == j, varis[0, 0, j], variance)
-    picked = jnp.concatenate(picked, axis=0)
-    cell_mean = jnp.sum(picked, axis=1, keepdims=True) * (1.0 / M)
-    factor = lax.rsqrt(variance)
-    lane4 = iota((4, CX), 1)
-    obs = jnp.where(lane4 < M - 1, picked, value)
-    obs = jnp.where(lane4 < M, (obs - cell_mean) * factor, 0.0)
-    rf[gx] = obs[0:2] + pltpu.roll(obs[2:4], M, 1)
+        row, place = lax.shift_right_logical(cell, 7), cell & (CX - 1)
+        column = jnp.sum(jnp.where(lane64 == place, zr[row], 0.0), axis=1, keepdims=True)
+        column = jnp.broadcast_to(column, (M, CX))
+        average = jnp.sum(column, axis=0, keepdims=True) * (1.0 / M)
+        factor = lax.rsqrt(ones + varis[0, 0, j])
+        values = jnp.sum(jnp.where(diag64, column, 0.0), axis=0, keepdims=True)
+        values = jnp.where(iota((1, CX), 1) < M - 1, values, ones + vals[0, 0, j])
+        picked.append(jnp.where(iota((1, CX), 1) < M, (values - average) * factor, 0.0))
+    rf[gx] = jnp.concatenate(
+        [picked[0] + pltpu.roll(picked[2], M, 1), picked[1] + pltpu.roll(picked[3], M, 1)], axis=0
+    )
 
     gx_copies = [
         pltpu.make_async_remote_copy(
@@ -256,10 +332,13 @@
         copy.start()
 
     for r in range(CY):
-        line = yb[pl.ds(r, M, stride=8), :] - mean[r:r + 1, :]
-        high = line.astype(BF16)
+        field = zr[r]
+        mean = jnp.sum(field, axis=0, keepdims=True) * (1.0 / M)
+        mean_ref[pl.ds(r, 1), :] = mean
+        field = field - mean
+        high = field.astype(BF16)
         hilo_ref[pl.ds(0, M), pl.ds(r * CX, CX)] = high
-        hilo_ref[pl.ds(M, M), pl.ds(r * CX, CX)] = (line - high.astype(F32)).astype(BF16)
+        hilo_ref[pl.ds(M, M), pl.ds(r * CX, CX)] = (field - high.astype(F32)).astype(BF16)
 
     wait_all(rf, ngx - 1, gx_recv)
     gathered = jnp.concatenate([rf[i] for i in range(ngx)], axis=0)
@@ -270,19 +349,9 @@
     gram = jnp.dot(rows.T, rows, precision=lax.Precision.HIGHEST, preferred_element_type=F32)
     gram_ref[...] = gram[0:32] + pltpu.roll(gram[32:64], M, 1)
 
-    for copy in side_halos:
-        copy.wait_send()
-
-    @pl.when(has_up)
-    def _():
-        for copy in up_halos:
-            copy.wait_send()
-
-    @pl.when(has_down)
-    def _():
-        for copy in down_halos:
-            copy.wait_send()
-
+    sent(up_rows, down_rows)
+    sent(up_flow, down_flow, side_flow)
+    sent(up_corners, down_corners, side_halos)
     wait_all(rf, ngx - 1, gx_send)
 
 
@@ -433,19 +502,25 @@
         out_specs=(vmem,) * 3,
         scratch_shapes=[
             pltpu.VMEM((M, CY, CX), F32),
+            pltpu.VMEM((CY + 2, M, CX), F32),
+            pltpu.VMEM((CY + 2, M, CX), F32),
+            pltpu.VMEM((CY, M, CX), F32),
             pltpu.VMEM((3, CY, CX), F32),
+            pltpu.VMEM((5, CY, CX), F32),
             pltpu.SMEM((1, 1, 4), jnp.int32),
             pltpu.SMEM((1, 1, 4), F32),
             pltpu.SMEM((1, 1, 4), F32),
-            pltpu.VMEM((24, CX), F32),
-            pltpu.VMEM((264, CX), F32),
-            pltpu.VMEM((512, CX), F32),
-            pltpu.VMEM((24, CX), F32),
-            pltpu.VMEM((24, CX), F32),
+            pltpu.VMEM((16, CX), F32),
+            pltpu.VMEM((2, 8, CX), F32),
+            pltpu.VMEM((2, M, CX), F32),
+            pltpu.VMEM((2, M, CX), F32),
+            pltpu.VMEM((16, CX), F32),
+            pltpu.VMEM((16, CX), F32),
             pltpu.VMEM((4, 16, CX), F32),
-            pltpu.VMEM((512, CX), F32),
+            pltpu.VMEM((4, 8, CX), F32),
+            pltpu.VMEM((2, 8, CX), F32),
             pltpu.VMEM((ngx, 2, CX), F32),
-            dma((5,)), dma((8,)), dma((8,)), dma, dma,
+            dma((13,)), dma((8,)), dma((8,)), dma((4,)), dma((4,)), dma, dma,
         ],
         compiler_params=pltpu.CompilerParams(collective_id=0, has_side_effects=True),
         name="forecast",

time: 44.4 us -> 42.4 us (0.955)
  Pallas kernels: 44.3 us -> 42.2 us
    pallas_call x1, Pallas kernels: 21.3 us -> 19.1 us  [body(): pl.pallas_call(functools.partial(forecast_kernel, ngy, ngx), out_shape=(p...]
where the time goes in v3:
time: 42.4 us; the launch traced here: 42.2 us
  Pallas kernels  42.2 us (100%)
    pallas_call x1, Pallas kernels, body(): pl.pallas_call(functools.partial(forecast_kernel, ngy, ngx), out_shape=(p...  19.1 us
    pallas_call x1, Pallas kernels, body(): pl.pallas_call(functools.partial(sum_kernel, ngy), out_shape=pltpu.VMEM((...  18.9 us
    pallas_call x1, Pallas kernels, body(): pl.pallas_call(analysis_kernel, out_shape=jax.ShapeDtypeStruct((M, CY, CX...  4.23 us

profile of v3, /device:TPU:1, one launch (start us, length us, event | category | flops | bytes accessed | tf_op | source)
XLA Modules:
  0.0 42.2 jit_solution(8757128731888824783)
XLA Ops:
  0.0 19.1 %forecast.1 = (f32[32,128]{1,0:T(8,128)S(1)}, bf16[128,1024]{1,0:T(8,128)(2,1)S(1)}, f32[8,128]{1,0:T(8,128)S(1)}) custom-call(f32[64,8,128]{2,1,0:T(8,128)} %x_hbm.1, f32[3,8,128]{2,1,0:T(8,128)} %flow_hbm.1, s32[1,1,4]{2,1,0:T(1,128)} %cell_hbm.1, f32[1,1,4]{2,1,0:T(1,128)} %val_hbm.1, f32[1,1,4]{2,1,0:T(1,128)} %var_hbm.1), custom_call_target="tpu_custom_call" | custom-call | tf_op jit(solution)/shard_map/forecast/pallas_call | solution.py:494
  19.1 18.9 %sums.1.gram_ref = f32[32,128]{1,0:T(8,128)S(1)} custom-call(f32[32,128]{1,0:T(8,128)S(1)} %get-tuple-element.8.part_ref), custom_call_target="tpu_custom_call" | custom-call | tf_op jit(solution)/shard_map/sums/pallas_call | solution.py:528
  38.0 4.2 %analysis.1 = f32[64,8,128]{2,1,0:T(8,128)} custom-call(f32[32,128]{1,0:T(8,128)S(1)} %sums.1.gram_ref, bf16[128,1024]{1,0:T(8,128)(2,1)S(1)} %get-tuple-element.9.hilo_ref, f32[8,128]{1,0:T(8,128)S(1)} %get-tuple-element.10.mean_ref), custom_call_target="tpu_custom_call" | custom-call | tf_op jit(solution)/shard_map/analysis/pallas_call | solution.py:541

commit v4 on v3

--- a/solution.py
+++ b/solution.py
@@ -37,7 +37,7 @@
     up, down = gy - 1, gy + 1
     has_up, has_down = gy > 0, gy < ngy - 1
     left, right = lax.rem(gx + ngx - 1, ngx), lax.rem(gx + 1, ngx)
-    gx_partners = [(gy, lax.rem(gx + i, ngx)) for i in range(1, ngx)]
+    gx_partners = [(gy, lax.rem(gx + i, ngx)) for i in sorted(range(1, ngx), key=lambda i: -min(i, ngx - i))]
 
     row_loads = [pltpu.make_async_copy(x_hbm.at[:, r, :], xr.at[r + 1], load_sem.at[5 + r]) for r in (0, 1, 6, 7, 2, 3, 4, 5)]
     flow_load = pltpu.make_async_copy(flow_hbm, fl, load_sem.at[1])
@@ -366,13 +366,15 @@
     nz = ngy // NX4
     zpos = gy // NX4
     xpos = lax.rem(gy, NX4)
+    core = lax.rem(gx, 2)
+    other = gx + 1 - 2 * core
     z_partners = [(lax.rem(gy + NX4 * i, ngy), gx) for i in range(1, nz)]
-    x_partners = [(zpos * NX4 + lax.rem(xpos + i, NX4), gx) for i in range(1, NX4)]
+    x_partners = [(zpos * NX4 + lax.rem(xpos + i, NX4), g) for i in (2, 1, 3) for g in (gx, other)] + [(gy, other)]
     barrier = pltpu.get_barrier_semaphore()
     for partner in z_partners + x_partners:
         pl.semaphore_signal(barrier, inc=1, device_id=partner, device_id_type=MESH)
-    rz[zpos] = part_ref[...]
-    pl.semaphore_wait(barrier, nz + NX4 - 2)
+    rz[zpos] = part_ref[pl.ds(pl.multiple_of(16 * core, 16), 16), :]
+    pl.semaphore_wait(barrier, nz - 1 + 2 * NX4 - 1)
 
     def spread(buffer, slot, partners, send, recv):
         for partner in partners:
@@ -383,15 +385,16 @@
 
     spread(rz, zpos, z_partners, z_send, z_recv)
     wait_all(rz, nz - 1, z_recv)
-    part = rz[0]
+    half = rz[0]
     for i in range(1, nz):
-        part = part + rz[i]
-    rx[xpos] = part
-    spread(rx, xpos, x_partners, x_send, x_recv)
-    wait_all(rx, NX4 - 1, x_recv)
-    gram_ref[...] = (rx[0] + rx[1]) + (rx[2] + rx[3])
+        half = half + rz[i]
+    rx[2 * xpos + core] = half
+    spread(rx, 2 * xpos + core, x_partners, x_send, x_recv)
+    wait_all(rx, 2 * NX4 - 1, x_recv)
+    for c in range(2):
+        gram_ref[pl.ds(16 * c, 16), :] = (rx[c] + rx[2 + c]) + (rx[4 + c] + rx[6 + c])
     wait_all(rz, nz - 1, z_send)
-    wait_all(rx, NX4 - 1, x_send)
+    wait_all(rx, 2 * NX4 - 1, x_send)
 
 
 def analysis_kernel(gram_ref, hilo_ref, mean_ref, out_ref):
@@ -402,6 +405,8 @@
     blocks = [packed[8 * i:8 * i + 8] for i in range(4)] + [shifted[8 * i:8 * i + 8] for i in range(4)]
     blocks = [jnp.where(lane < M - 1, b, 0.0) for b in blocks]
     row_sums = [jnp.sum(b, axis=1, keepdims=True) for b in blocks]
+    eyes = [lane == sub + 8 * i for i in range(8)]
+    diagonals = [jnp.where(e, b, 0.0) for e, b in zip(eyes, blocks)]
     last = sub == 7
     target_row = blocks[7][7:8] + jnp.where(lane[0:1] == M - 1, -row_sums[7][7:8], 0.0)
     blocks[7] = jnp.where(last, 0.0, blocks[7])
@@ -411,11 +416,12 @@
     all_sum = jnp.sum(functools.reduce(jnp.add, row_sums), axis=0, keepdims=True)
     blocks = [jnp.where(lane == M - 1, -r, b) for b, r in zip(blocks, row_sums)]
     blocks[7] = jnp.where(last, jnp.where(lane == M - 1, all_sum, -col_sum), blocks[7])
-    eyes = [lane == sub + 8 * i for i in range(8)]
+    scale_row = jnp.sum(functools.reduce(jnp.add, diagonals), axis=0, keepdims=True)
+    scale_row = lax.rsqrt((M - 1.0) + jnp.where(lane[0:1] == M - 1, all_sum, scale_row))
+    scale_col = [jnp.sum(d, axis=1, keepdims=True) for d in diagonals]
+    scale_col[7] = jnp.where(last[:, 0:1], all_sum, scale_col[7])
+    scale_col = [lax.rsqrt((M - 1.0) + c) for c in scale_col]
     blocks = [jnp.where(e, b + (M - 1.0), b) for e, b in zip(eyes, blocks)]
-    diagonals = [jnp.where(e, b, 0.0) for e, b in zip(eyes, blocks)]
-    scale_row = lax.rsqrt(jnp.sum(functools.reduce(jnp.add, diagonals), axis=0, keepdims=True) + jnp.where(lane[0:1] < M, 0.0, 1.0))
-    scale_col = [lax.rsqrt(jnp.sum(d, axis=1, keepdims=True)) for d in diagonals]
     a = [
         jnp.where(lane == sub + (M + 8 * i), scale_col[i], jnp.where(lane < M, blocks[i] * scale_col[i] * scale_row, 0.0))
         for i in range(8)
@@ -531,8 +537,8 @@
         in_specs=[vmem],
         out_specs=vmem,
         scratch_shapes=[
-            pltpu.VMEM((ngy // NX4, 32, CX), F32),
-            pltpu.VMEM((NX4, 32, CX), F32),
+            pltpu.VMEM((ngy // NX4, 16, CX), F32),
+            pltpu.VMEM((2 * NX4, 16, CX), F32),
             dma, dma, dma, dma,
         ],
         compiler_params=pltpu.CompilerParams(collective_id=1, has_side_effects=True),

time: 42.4 us -> 42.2 us (level)
  no operation moved by 1% of the time
where the time goes in v4:
time: 42.2 us; the launch traced here: 42 us
  Pallas kernels  42 us (100%)
    pallas_call x1, Pallas kernels, body(): pl.pallas_call(functools.partial(forecast_kernel, ngy, ngx), out_shape=(p...  18.9 us
    pallas_call x1, Pallas kernels, body(): pl.pallas_call(functools.partial(sum_kernel, ngy), out_shape=pltpu.VMEM((...  18.9 us
    pallas_call x1, Pallas kernels, body(): pl.pallas_call(analysis_kernel, out_shape=jax.ShapeDtypeStruct((M, CY, CX...  4.22 us

profile of v4, /device:TPU:1, one launch (start us, length us, event | category | flops | bytes accessed | tf_op | source)
XLA Modules:
  0.0 42.0 jit_solution(16065063401818241459)
XLA Ops:
  0.0 18.9 %forecast.1 = (f32[32,128]{1,0:T(8,128)S(1)}, bf16[128,1024]{1,0:T(8,128)(2,1)S(1)}, f32[8,128]{1,0:T(8,128)S(1)}) custom-call(f32[64,8,128]{2,1,0:T(8,128)} %x_hbm.1, f32[3,8,128]{2,1,0:T(8,128)} %flow_hbm.1, s32[1,1,4]{2,1,0:T(1,128)} %cell_hbm.1, f32[1,1,4]{2,1,0:T(1,128)} %val_hbm.1, f32[1,1,4]{2,1,0:T(1,128)} %var_hbm.1), custom_call_target="tpu_custom_call" | custom-call | tf_op jit(solution)/shard_map/forecast/pallas_call | solution.py:500
  18.9 18.9 %sums.1.gram_ref = f32[32,128]{1,0:T(8,128)S(1)} custom-call(f32[32,128]{1,0:T(8,128)S(1)} %get-tuple-element.8.part_ref), custom_call_target="tpu_custom_call" | custom-call | tf_op jit(solution)/shard_map/sums/pallas_call | solution.py:534
  37.8 4.2 %analysis.1 = f32[64,8,128]{2,1,0:T(8,128)} custom-call(f32[32,128]{1,0:T(8,128)S(1)} %sums.1.gram_ref, bf16[128,1024]{1,0:T(8,128)(2,1)S(1)} %get-tuple-element.9.hilo_ref, f32[8,128]{1,0:T(8,128)S(1)} %get-tuple-element.10.mean_ref), custom_call_target="tpu_custom_call" | custom-call | tf_op jit(solution)/shard_map/analysis/pallas_call | solution.py:547

commit v5 on v3

--- a/solution.py
+++ b/solution.py
@@ -37,7 +37,7 @@
     up, down = gy - 1, gy + 1
     has_up, has_down = gy > 0, gy < ngy - 1
     left, right = lax.rem(gx + ngx - 1, ngx), lax.rem(gx + 1, ngx)
-    gx_partners = [(gy, lax.rem(gx + i, ngx)) for i in range(1, ngx)]
+    gx_partners = [(gy, lax.rem(gx + i, ngx)) for i in sorted(range(1, ngx), key=lambda i: -min(i, ngx - i))]
 
     row_loads = [pltpu.make_async_copy(x_hbm.at[:, r, :], xr.at[r + 1], load_sem.at[5 + r]) for r in (0, 1, 6, 7, 2, 3, 4, 5)]
     flow_load = pltpu.make_async_copy(flow_hbm, fl, load_sem.at[1])
@@ -347,7 +347,12 @@
         [jnp.where(lane32 < M, gathered, 0.0), jnp.where(lane32 < M, pltpu.roll(gathered, M, 1), 0.0)], axis=0
     )
     gram = jnp.dot(rows.T, rows, precision=lax.Precision.HIGHEST, preferred_element_type=F32)
-    gram_ref[...] = gram[0:32] + pltpu.roll(gram[32:64], M, 1)
+    high, low = gram[0:32], pltpu.roll(gram[32:64], CX - 32, 1)
+    across, along = iota((32, CX), 1), iota((32, CX), 0)
+    square = jnp.where((across < 32) & (across > along), low, high)
+    gram_ref[pl.ds(0, 16), :] = square[0:16] + pltpu.roll(square[16:32], M, 1)
+    diagonal = jnp.sum(jnp.where(across == along, low, 0.0), axis=0, keepdims=True)
+    gram_ref[pl.ds(16, 8), :] = jnp.where(iota((8, CX), 0) == 0, diagonal, 0.0)
 
     sent(up_rows, down_rows)
     sent(up_flow, down_flow, side_flow)
@@ -367,41 +372,54 @@
     zpos = gy // NX4
     xpos = lax.rem(gy, NX4)
     z_partners = [(lax.rem(gy + NX4 * i, ngy), gx) for i in range(1, nz)]
-    x_partners = [(zpos * NX4 + lax.rem(xpos + i, NX4), gx) for i in range(1, NX4)]
+    x_partners = [(zpos * NX4 + lax.rem(xpos + i, NX4), gx) for i in (2, 1, 3)]
     barrier = pltpu.get_barrier_semaphore()
     for partner in z_partners + x_partners:
         pl.semaphore_signal(barrier, inc=1, device_id=partner, device_id_type=MESH)
     rz[zpos] = part_ref[...]
     pl.semaphore_wait(barrier, nz + NX4 - 2)
 
+    def wait_rows(buffer, count, sem):
+        piece = buffer.at[pl.ds(0, count), pl.ds(0, 17)]
+        pltpu.make_async_copy(piece, piece, sem).wait()
+
     def spread(buffer, slot, partners, send, recv):
         for partner in partners:
             pltpu.make_async_remote_copy(
-                src_ref=buffer.at[slot], dst_ref=buffer.at[slot], send_sem=send, recv_sem=recv,
+                src_ref=buffer.at[slot, pl.ds(0, 17)], dst_ref=buffer.at[slot, pl.ds(0, 17)], send_sem=send, recv_sem=recv,
                 device_id=partner, device_id_type=MESH,
             ).start()
 
     spread(rz, zpos, z_partners, z_send, z_recv)
-    wait_all(rz, nz - 1, z_recv)
+    wait_rows(rz, nz - 1, z_recv)
     part = rz[0]
     for i in range(1, nz):
         part = part + rz[i]
     rx[xpos] = part
     spread(rx, xpos, x_partners, x_send, x_recv)
-    wait_all(rx, NX4 - 1, x_recv)
+    wait_rows(rx, NX4 - 1, x_recv)
     gram_ref[...] = (rx[0] + rx[1]) + (rx[2] + rx[3])
-    wait_all(rz, nz - 1, z_send)
-    wait_all(rx, NX4 - 1, x_send)
+    wait_rows(rz, nz - 1, z_send)
+    wait_rows(rx, NX4 - 1, x_send)
 
 
 def analysis_kernel(gram_ref, hilo_ref, mean_ref, out_ref):
     lane = iota((8, CX), 1)
     sub = iota((8, CX), 0)
-    packed = gram_ref[...]
-    shifted = pltpu.roll(packed, M, 1)
-    blocks = [packed[8 * i:8 * i + 8] for i in range(4)] + [shifted[8 * i:8 * i + 8] for i in range(4)]
+    packed = gram_ref[pl.ds(0, 16), :]
+    square = jnp.concatenate([packed, pltpu.roll(packed, M, 1)], axis=0)
+    square = jnp.where(iota((32, CX), 1) < M, square, 0.0)
+    turned = jnp.concatenate([square, jnp.zeros((CX - 32, CX), F32)], axis=0).T
+    across, along = iota((32, CX), 1), iota((32, CX), 0)
+    top = jnp.where((across < 32) & (across > along), turned[0:32], square)
+    corner = jnp.where(across > along, square, jnp.where(across == along, gram_ref[pl.ds(16, 1), :], turned[0:32]))
+    corner = pltpu.roll(jnp.where(across < 32, corner, 0.0), 32, 1)
+    bottom = jnp.where(across < 32, turned[32:64], corner)
+    blocks = [top[8 * i:8 * i + 8] for i in range(4)] + [bottom[8 * i:8 * i + 8] for i in range(4)]
     blocks = [jnp.where(lane < M - 1, b, 0.0) for b in blocks]
     row_sums = [jnp.sum(b, axis=1, keepdims=True) for b in blocks]
+    eyes = [lane == sub + 8 * i for i in range(8)]
+    diagonals = [jnp.where(e, b, 0.0) for e, b in zip(eyes, blocks)]
     last = sub == 7
     target_row = blocks[7][7:8] + jnp.where(lane[0:1] == M - 1, -row_sums[7][7:8], 0.0)
     blocks[7] = jnp.where(last, 0.0, blocks[7])
@@ -411,11 +429,12 @@
     all_sum = jnp.sum(functools.reduce(jnp.add, row_sums), axis=0, keepdims=True)
     blocks = [jnp.where(lane == M - 1, -r, b) for b, r in zip(blocks, row_sums)]
     blocks[7] = jnp.where(last, jnp.where(lane == M - 1, all_sum, -col_sum), blocks[7])
-    eyes = [lane == sub + 8 * i for i in range(8)]
+    scale_row = jnp.sum(functools.reduce(jnp.add, diagonals), axis=0, keepdims=True)
+    scale_row = lax.rsqrt((M - 1.0) + jnp.where(lane[0:1] == M - 1, all_sum, scale_row))
+    scale_col = [jnp.sum(d, axis=1, keepdims=True) for d in diagonals]
+    scale_col[7] = jnp.where(last[:, 0:1], all_sum, scale_col[7])
+    scale_col = [lax.rsqrt((M - 1.0) + c) for c in scale_col]
     blocks = [jnp.where(e, b + (M - 1.0), b) for e, b in zip(eyes, blocks)]
-    diagonals = [jnp.where(e, b, 0.0) for e, b in zip(eyes, blocks)]
-    scale_row = lax.rsqrt(jnp.sum(functools.reduce(jnp.add, diagonals), axis=0, keepdims=True) + jnp.where(lane[0:1] < M, 0.0, 1.0))
-    scale_col = [lax.rsqrt(jnp.sum(d, axis=1, keepdims=True)) for d in diagonals]
     a = [
         jnp.where(lane == sub + (M + 8 * i), scale_col[i], jnp.where(lane < M, blocks[i] * scale_col[i] * scale_row, 0.0))
         for i in range(8)
@@ -494,7 +513,7 @@
     part, hilo, mean = pl.pallas_call(
         functools.partial(forecast_kernel, ngy, ngx),
         out_shape=(
-            pltpu.VMEM((32, CX), F32),
+            pltpu.VMEM((24, CX), F32),
             pltpu.VMEM((2 * M, CY * CX), BF16),
             pltpu.VMEM((CY, CX), F32),
         ),
@@ -527,12 +546,12 @@
     )(ensemble, flow, obs_cell, obs_value, obs_var)
     gram = pl.pallas_call(
         functools.partial(sum_kernel, ngy),
-        out_shape=pltpu.VMEM((32, CX), F32),
+        out_shape=pltpu.VMEM((24, CX), F32),
         in_specs=[vmem],
         out_specs=vmem,
         scratch_shapes=[
-            pltpu.VMEM((ngy // NX4, 32, CX), F32),
-            pltpu.VMEM((NX4, 32, CX), F32),
+            pltpu.VMEM((ngy // NX4, 24, CX), F32),
+            pltpu.VMEM((NX4, 24, CX), F32),
             dma, dma, dma, dma,
         ],
         compiler_params=pltpu.CompilerParams(collective_id=1, has_side_effects=True),

time: 42.4 us -> 40.8 us (0.962)
  Pallas kernels: 42.2 us -> 40.5 us
    pallas_call x1, Pallas kernels: 18.9 us -> 17.2 us  [body(): pl.pallas_call(functools.partial(sum_kernel, ngy), out_shape=pltpu.VMEM((...]
where the time goes in v5:
time: 40.8 us; the launch traced here: 40.5 us
  Pallas kernels  40.5 us (99%)
    pallas_call x1, Pallas kernels, body(): pl.pallas_call(functools.partial(forecast_kernel, ngy, ngx), out_shape=(p...  19 us
    pallas_call x1, Pallas kernels, body(): pl.pallas_call(functools.partial(sum_kernel, ngy), out_shape=pltpu.VMEM((...  17.2 us
    pallas_call x1, Pallas kernels, body(): pl.pallas_call(analysis_kernel, out_shape=jax.ShapeDtypeStruct((M, CY, CX...  4.35 us

profile of v5, /device:TPU:1, one launch (start us, length us, event | category | flops | bytes accessed | tf_op | source)
XLA Modules:
  0.0 40.5 jit_solution(8503830097456352928)
XLA Ops:
  0.0 19.0 %forecast.1 = (f32[24,128]{1,0:T(8,128)S(1)}, bf16[128,1024]{1,0:T(8,128)(2,1)S(1)}, f32[8,128]{1,0:T(8,128)S(1)}) custom-call(f32[64,8,128]{2,1,0:T(8,128)} %x_hbm.1, f32[3,8,128]{2,1,0:T(8,128)} %flow_hbm.1, s32[1,1,4]{2,1,0:T(1,128)} %cell_hbm.1, f32[1,1,4]{2,1,0:T(1,128)} %val_hbm.1, f32[1,1,4]{2,1,0:T(1,128)} %var_hbm.1), custom_call_target="tpu_custom_call" | custom-call | tf_op jit(solution)/shard_map/forecast/pallas_call | solution.py:513
  19.0 17.2 %sums.1.gram_ref = f32[24,128]{1,0:T(8,128)S(1)} custom-call(f32[24,128]{1,0:T(8,128)S(1)} %get-tuple-element.8.part_ref), custom_call_target="tpu_custom_call" | custom-call | tf_op jit(solution)/shard_map/sums/pallas_call | solution.py:547
  36.2 4.3 %analysis.1 = f32[64,8,128]{2,1,0:T(8,128)} custom-call(f32[24,128]{1,0:T(8,128)S(1)} %sums.1.gram_ref, bf16[128,1024]{1,0:T(8,128)(2,1)S(1)} %get-tuple-element.9.hilo_ref, f32[8,128]{1,0:T(8,128)S(1)} %get-tuple-element.10.mean_ref), custom_call_target="tpu_custom_call" | custom-call | tf_op jit(solution)/shard_map/analysis/pallas_call | solution.py:560

commit v6 on v5

--- a/solution.py
+++ b/solution.py
@@ -403,7 +403,7 @@
     wait_rows(rx, NX4 - 1, x_send)
 
 
-def analysis_kernel(gram_ref, hilo_ref, mean_ref, out_ref):
+def analysis_kernel(gram_ref, hilo_ref, mean_ref, out_hbm, rows_out, out_sem):
     lane = iota((8, CX), 1)
     sub = iota((8, CX), 0)
     packed = gram_ref[pl.ds(0, 16), :]
@@ -441,11 +441,13 @@
     ]
 
     lower = [None] * 8
+    nothing = 0.0 * packed[0:8]
     for p in range(16):
         b, o = p // 2, 4 * (p % 2)
         cols = {
             (t, i): jnp.broadcast_to(a[i][:, 4 * p + t:4 * p + t + 1], (8, CX)) for t in range(4) for i in range(b, 8)
         }
+        cols = {key: v + nothing if key[1] == b else v for key, v in cols.items()}
         d = {
             (s, t): jnp.broadcast_to(cols[t, b][o + s:o + s + 1, :], (8, CX)) for s in range(4) for t in range(s + 1)
         }
@@ -498,8 +500,11 @@
         block = hilo_ref[:, cols]
         right = jnp.concatenate([block, block], axis=0)
         res = jnp.dot(left, right, preferred_element_type=F32)
-        out_ref[:, r, :] = res[:, :CX] + mean_ref[r:r + 1, :]
-        out_ref[:, r + 1, :] = res[:, CX:] + mean_ref[r + 1:r + 2, :]
+        for half in range(2):
+            rows_out[r + half] = res[:, half * CX:(half + 1) * CX] + mean_ref[r + half:r + half + 1, :]
+            pltpu.make_async_copy(rows_out.at[r + half], out_hbm.at[:, r + half, :], out_sem.at[r + half]).start()
+    for r in range(CY):
+        pltpu.make_async_copy(rows_out.at[r], out_hbm.at[:, r, :], out_sem.at[r]).wait()
 
 
 def near(array):
@@ -561,7 +566,8 @@
         analysis_kernel,
         out_shape=jax.ShapeDtypeStruct((M, CY, CX), F32),
         in_specs=[vmem] * 3,
-        out_specs=vmem,
+        out_specs=hbm,
+        scratch_shapes=[pltpu.VMEM((CY, M, CX), F32), dma((CY,))],
         name="analysis",
     )(near(gram), near(hilo), near(mean))
 

time: 40.8 us -> 39.9 us (0.978)
  Pallas kernels: 40.5 us -> 39.7 us
    pallas_call x1, Pallas kernels: 4.35 us -> 3.5 us  [body(): pl.pallas_call(analysis_kernel, out_shape=jax.ShapeDtypeStruct((M, CY, CX...]
where the time goes in v6:
time: 39.9 us; the launch traced here: 39.7 us
  Pallas kernels  39.7 us (99%)
    pallas_call x1, Pallas kernels, body(): pl.pallas_call(functools.partial(forecast_kernel, ngy, ngx), out_shape=(p...  19 us
    pallas_call x1, Pallas kernels, body(): pl.pallas_call(functools.partial(sum_kernel, ngy), out_shape=pltpu.VMEM((...  17.2 us
    pallas_call x1, Pallas kernels, body(): pl.pallas_call(analysis_kernel, out_shape=jax.ShapeDtypeStruct((M, CY, CX...  3.5 us

profile of v6, /device:TPU:1, one launch (start us, length us, event | category | flops | bytes accessed | tf_op | source)
XLA Modules:
  0.0 39.7 jit_solution(3180165165125548149)
XLA Ops:
  0.0 19.0 %forecast.1 = (f32[24,128]{1,0:T(8,128)S(1)}, bf16[128,1024]{1,0:T(8,128)(2,1)S(1)}, f32[8,128]{1,0:T(8,128)S(1)}) custom-call(f32[64,8,128]{2,1,0:T(8,128)} %x_hbm.1, f32[3,8,128]{2,1,0:T(8,128)} %flow_hbm.1, s32[1,1,4]{2,1,0:T(1,128)} %cell_hbm.1, f32[1,1,4]{2,1,0:T(1,128)} %val_hbm.1, f32[1,1,4]{2,1,0:T(1,128)} %var_hbm.1), custom_call_target="tpu_custom_call" | custom-call | tf_op jit(solution)/shard_map/forecast/pallas_call | solution.py:518
  19.0 17.2 %sums.1.gram_ref = f32[24,128]{1,0:T(8,128)S(1)} custom-call(f32[24,128]{1,0:T(8,128)S(1)} %get-tuple-element.8.part_ref), custom_call_target="tpu_custom_call" | custom-call | tf_op jit(solution)/shard_map/sums/pallas_call | solution.py:552
  36.2 3.5 %analysis.1 = f32[64,8,128]{2,1,0:T(8,128)} custom-call(f32[24,128]{1,0:T(8,128)S(1)} %sums.1.gram_ref, bf16[128,1024]{1,0:T(8,128)(2,1)S(1)} %get-tuple-element.9.hilo_ref, f32[8,128]{1,0:T(8,128)S(1)} %get-tuple-element.10.mean_ref), custom_call_target="tpu_custom_call" | custom-call | tf_op jit(solution)/shard_map/analysis/pallas_call | solution.py:565

commit v7 on v6

--- a/solution.py
+++ b/solution.py
@@ -29,8 +29,8 @@
     ngy, ngx,
     x_hbm, flow_hbm, cell_hbm, val_hbm, var_hbm,
     gram_ref, hilo_ref, mean_ref,
-    xb, xr, yr, zr, fl, cf, cells, vals, varis, qs, fs, hu_rows, hd_rows, hl, hr, kb, fh, zc, rf,
-    load_sem, halo_send, halo_recv, flow_send, flow_recv, gx_send, gx_recv,
+    xb, xr, yr, zr, fl, cf, cells, obs, qs, fs, ct, h_rows, h_sides, h_corners, fh, zc, rf,
+    load_sem, halo_send, halo_recv, gx_send, gx_recv,
 ):
     gy = lax.axis_index("gy")
     gx = lax.axis_index("gx")
@@ -39,17 +39,21 @@
     left, right = lax.rem(gx + ngx - 1, ngx), lax.rem(gx + 1, ngx)
     gx_partners = [(gy, lax.rem(gx + i, ngx)) for i in sorted(range(1, ngx), key=lambda i: -min(i, ngx - i))]
 
-    row_loads = [pltpu.make_async_copy(x_hbm.at[:, r, :], xr.at[r + 1], load_sem.at[5 + r]) for r in (0, 1, 6, 7, 2, 3, 4, 5)]
-    flow_load = pltpu.make_async_copy(flow_hbm, fl, load_sem.at[1])
-    loads = [
-        pltpu.make_async_copy(x_hbm, xb, load_sem.at[0]),
-        pltpu.make_async_copy(cell_hbm, cells, load_sem.at[2]),
-        pltpu.make_async_copy(val_hbm, vals, load_sem.at[3]),
-        pltpu.make_async_copy(var_hbm, varis, load_sem.at[4]),
-    ]
-    flow_load.start()
-    for copy in row_loads + loads:
-        copy.start()
+    def load(src, dst, index):
+        pltpu.make_async_copy(src, dst, load_sem.at[index]).start()
+
+    def loaded(piece, index):
+        pltpu.make_async_copy(piece, piece, load_sem.at[index]).wait()
+
+    load(flow_hbm, fl, 0)
+    for r in (0, 7, 1, 6):
+        load(x_hbm.at[:, r, :], xr.at[r + 1], 1)
+    load(x_hbm, xb, 2)
+    for r in (2, 3, 4, 5):
+        load(x_hbm.at[:, r, :], xr.at[r + 1], 3)
+    load(cell_hbm, cells, 4)
+    load(val_hbm, obs.at[0], 5)
+    load(var_hbm, obs.at[1], 5)
     barrier = pltpu.get_barrier_semaphore()
 
     def greet(partners):
@@ -75,67 +79,46 @@
     q0, q1, q3 = quad == 0, quad == 1, quad == 3
     west_side = quad >= 2
 
-    def remote(src, dst, index, target, send=halo_send, recv=halo_recv):
+    def remote(src, dst, index, target):
         return pltpu.make_async_remote_copy(
-            src_ref=src, dst_ref=dst, send_sem=send.at[index], recv_sem=recv.at[index],
+            src_ref=src, dst_ref=dst, send_sem=halo_send.at[index], recv_sem=halo_recv.at[index],
             device_id=target, device_id_type=MESH,
         )
 
-    up_flow = [remote(fs.at[0], fh.at[0], 0, (up, gx), flow_send, flow_recv)]
-    down_flow = [remote(fs.at[0], fh.at[1], 1, (down, gx), flow_send, flow_recv)]
-    side_flow = [
-        remote(fs.at[1], fh.at[2], 2, (gy, left), flow_send, flow_recv),
-        remote(fs.at[1], fh.at[3], 3, (gy, right), flow_send, flow_recv),
-    ]
-    up_rows = [remote(xr.at[pl.ds(1, 2)], hd_rows, 0, (up, gx))]
-    down_rows = [remote(xr.at[pl.ds(7, 2)], hu_rows, 1, (down, gx))]
-    up_corners = [remote(qs, kb.at[0], 4, (up, left)), remote(qs, kb.at[1], 5, (up, right))]
-    down_corners = [remote(qs, kb.at[2], 6, (down, left)), remote(qs, kb.at[3], 7, (down, right))]
-    side_halos = [remote(qs, hr, 2, (gy, left)), remote(qs, hl, 3, (gy, right))]
-
-    def start(up_copies, down_copies, side_copies=()):
+    def start(index, to_up, to_down, to_left=None, to_right=None):
         @pl.when(has_up)
         def _():
-            for copy in up_copies:
-                copy.start()
+            for src, dst, target in to_up:
+                remote(src, dst, index, (up, target)).start()
 
         @pl.when(has_down)
         def _():
-            for copy in down_copies:
-                copy.start()
-
-        for copy in side_copies:
-            copy.start()
-
-    def received(up_copies, down_copies, side_copies=()):
-        for copy in side_copies:
-            copy.wait_recv()
-
-        @pl.when(has_up)
-        def _():
-            for copy in down_copies:
-                copy.wait_recv()
-
-        @pl.when(has_down)
-        def _():
-            for copy in up_copies:
-                copy.wait_recv()
-
-    def sent(up_copies, down_copies, side_copies=()):
-        for copy in side_copies:
-            copy.wait_send()
-
-        @pl.when(has_up)
-        def _():
-            for copy in up_copies:
-                copy.wait_send()
-
-        @pl.when(has_down)
-        def _():
-            for copy in down_copies:
-                copy.wait_send()
-
-    flow_load.wait()
+            for src, dst, target in to_down:
+                remote(src, dst, index, (down, target)).start()
+
+        if to_left:
+            remote(*to_left, index, (gy, left)).start()
+            remote(*to_right, index, (gy, right)).start()
+
+    both = has_up & has_down
+
+    def settle(sem, buffer, most, least):
+        def wait(count):
+            piece = buffer.at[pl.ds(0, count)]
+            pltpu.make_async_copy(piece, piece, sem).wait()
+
+        if most == least:
+            wait(most)
+        else:
+            pl.when(both)(lambda: wait(most))
+            pl.when(jnp.logical_not(both))(lambda: wait(least))
+
+    groups = [(fh, 4, 3), (h_sides, 2, 2), (h_rows, 4, 2), (h_corners, 4, 2)]
+
+    def received(index):
+        settle(halo_recv.at[index], *groups[index])
+
+    loaded(fl, 0)
     qc = jnp.where(edge, fl[0], 0.0)
     for i in range(1, 3):
         qc = qc + pltpu.roll(jnp.where(edge, fl[i], 0.0), 4 * i, 1)
@@ -143,21 +126,31 @@
     for i in range(3):
         fs[0, pl.ds(i, 1), :] = fl[i, 0:1, :]
         fs[0, pl.ds(3 + i, 1), :] = fl[i, 7:8, :]
-    for copy in row_loads[:4]:
-        copy.wait()
-
-    @pl.when(has_up & has_down)
+    loaded(xr.at[pl.ds(0, 4)], 1)
+
+    @pl.when(both)
     def _():
         pl.semaphore_wait(barrier, ngx + 5)
 
-    @pl.when(jnp.logical_not(has_up & has_down))
+    @pl.when(jnp.logical_not(both))
     def _():
         pl.semaphore_wait(barrier, ngx + 2)
 
-    start(up_rows, down_rows)
-    start(up_flow, down_flow, side_flow)
-    for copy in row_loads[4:] + loads:
-        copy.wait()
+    start(2, [(xr.at[pl.ds(1, 2)], h_rows.at[pl.ds(2, 2)], gx)], [(xr.at[pl.ds(7, 2)], h_rows.at[pl.ds(0, 2)], gx)])
+    start(0, [(fs.at[0], fh.at[1], gx)], [(fs.at[0], fh.at[0], gx)], (fs.at[1], fh.at[2]), (fs.at[1], fh.at[3]))
+    ends = l0 | l127
+    tile = jnp.zeros((8, CX), F32)
+    for b in range(8):
+        rows = pl.ds(8 * b, 8)
+        tile = tile + pltpu.roll(jnp.where(ends, xr[1, rows, :], 0.0), 4 * b, 1)
+        tile = tile + pltpu.roll(jnp.where(ends, xr[8, rows, :], 0.0), 4 * b + 2, 1)
+    ct[...] = tile
+    start(
+        3,
+        [(ct, h_corners.at[3], left), (ct, h_corners.at[2], right)],
+        [(ct, h_corners.at[1], left), (ct, h_corners.at[0], right)],
+    )
+    loaded(xb, 2)
 
     def pack(half):
         def body(i, q):
@@ -170,7 +163,10 @@
     qa, qb = pack(0), pack(1)
     qs[pl.ds(0, 8), :] = qa
     qs[pl.ds(8, 8), :] = qb
-    start(up_corners, down_corners, side_halos)
+    start(1, [], [], (qs, h_sides.at[0]), (qs, h_sides.at[1]))
+    loaded(xr.at[pl.ds(0, 4)], 3)
+    loaded(cells, 4)
+    loaded(obs, 5)
 
     def weights(f0, f1, f2):
         hu, hv = 0.5 * f1, 0.5 * f2
@@ -218,10 +214,9 @@
     def on(flag):
         return jnp.full((8, CX), jnp.where(flag, 1, 0), jnp.int32) > 0
 
-    hmask = (s7 & on(has_up)) | (s0 & on(has_down))
     cmask = (west_side & on(has_left)) | ((quad <= 1) & on(has_right))
 
-    received(up_flow, down_flow, side_flow)
+    received(0)
 
     def flow_cols(i):
         west, east = col(fh[3], (4 * i - 1) % CX), col(fh[2], 4 * i)
@@ -236,62 +231,68 @@
     def line(v, r):
         return jnp.broadcast_to(v[r:r + 1, :], (8, CX))
 
+    ends_in = (l0 & on(has_left)) | (l127 & on(has_right))
+
+    def beside(i):
+        return jnp.where(l0, pltpu.roll(fh[3], (1 - 4 * i) % CX, 1), pltpu.roll(fh[2], CX - 1 - 4 * i, 1))
+
+    k_side, v_side = beside(0), 0.5 * beside(2)
+
     def outside(above):
         if above:
-            t0, tn, ts, tw, te = outer_row(fh[1], 3, has_up)
+            t0, tn, ts, tw, te = outer_row(fh[0], 3, has_up)
             r, near, far, cross, toward = 0, line(an, 0), tn, ts, line(an, 1)
+            side = line(k_side + v_side, 0)
         else:
-            t0, tn, ts, tw, te = outer_row(fh[0], 0, has_down)
+            t0, tn, ts, tw, te = outer_row(fh[1], 0, has_down)
             r, near, far, cross, toward = 7, line(as_, 7), ts, tn, line(as_, 6)
+            side = line(k_side - v_side, 7)
         west = near * jnp.where(l0, 0.0, tw) + line(aw_in, r) * pltpu.roll(near, 1, 1)
         east = near * jnp.where(l127, 0.0, te) + line(ae_in, r) * pltpu.roll(near, CX - 1, 1)
-        corner = jnp.where(q0, col(near * tw, 0), jnp.where(q3, col(near * te, CX - 1), 0.0))
-        return (near * (t0 + line(a0, r)), near * far, near * cross, west, east, toward * near), corner
-
-    above, corner_above = outside(True)
-    below, corner_below = outside(False)
-    c_corner = jnp.where(s0, corner_above, jnp.where(s7, corner_below, 0.0))
-
-    received(up_corners, down_corners, side_halos)
+        corner = jnp.where(l0, near * tw + line(aw, r) * side, near * te + line(ae, r) * side)
+        corner = jnp.where(ends_in, corner, 0.0)
+        return near * (t0 + line(a0, r)), near * far, near * cross, west, east, toward * near, corner
+
+    above = outside(True)
+    below = outside(False)
+
+    received(1)
     west_cell = q3
     for half in range(2):
         q = (qa, qb)[half]
         rows = pl.ds(8 * half, 8)
-        ring = jnp.where(cmask, jnp.where(west_side, hl[rows, :], hr[rows, :]), 0.0)
-        corner_w = jnp.where(s7, kb[3, rows, :], kb[1, rows, :])
-        corner_e = jnp.where(s7, kb[2, rows, :], kb[0, rows, :])
-        corner = jnp.where(hmask & cmask, jnp.where(west_side, corner_w, corner_e), 0.0)
-        n = pltpu.roll(jnp.where(s7, corner, ring), 1, 0)
-        s = pltpu.roll(jnp.where(s0, corner, ring), 7, 0)
+        ring = jnp.where(cmask, jnp.where(west_side, h_sides[1, rows, :], h_sides[0, rows, :]), 0.0)
+        n = pltpu.roll(jnp.where(s7, 0.0, ring), 1, 0)
+        s = pltpu.roll(jnp.where(s0, 0.0, ring), 7, 0)
         ring_w, ring_e = pltpu.roll(ring, 1, 1), pltpu.roll(ring, CX - 1, 1)
         w = jnp.where(west_cell, ring_w, pltpu.roll(q, 1, 1))
         e = jnp.where(west_cell, pltpu.roll(q, CX - 1, 1), ring_e)
         ring1 = step(ring, n, s, w, e, kc, uc, vc)
         x1 = jnp.where(q0, ring_w, ring_e)
         y1 = jnp.where(q0, pltpu.roll(ring1, 1, 1), pltpu.roll(ring1, CX - 1, 1))
-        outer = jnp.where(s0, pltpu.roll(corner, 1, 0), pltpu.roll(corner, 7, 0))
-        outer = jnp.where(q0, pltpu.roll(outer, 1, 1), pltpu.roll(outer, CX - 1, 1))
         d = c_edge * x1
-        at_edge = a0_edge * d + an_edge * pltpu.roll(d, 1, 0) + as_edge * pltpu.roll(d, 7, 0) + c_edge * y1 + c_corner * outer
+        at_edge = a0_edge * d + an_edge * pltpu.roll(d, 1, 0) + as_edge * pltpu.roll(d, 7, 0) + c_edge * y1
         inside = c_next * jnp.where(q1, pltpu.roll(d, 1, 1), pltpu.roll(d, CX - 1, 1))
         zc[half] = jnp.where(q0 | q3, at_edge, inside)
 
-    received(up_rows, down_rows)
-
-    def add_rows(flag, c, near_row, far_row, r, r_in):
+    received(2)
+    received(3)
+
+    def add_rows(flag, c, near_row, far_row, r, r_in, corners, first):
         @pl.when(flag)
         def _():
+            merged = corners()
             for b in range(8):
                 rows = pl.ds(8 * b, 8)
-                p = near_row[rows, :]
+                p = h_rows[near_row, rows, :]
                 zr[r, rows, :] = zr[r, rows, :] + (
-                    (c[0] * p + c[1] * far_row[rows, :]) + (c[2] * xr[r + 1, rows, :] + c[3] * pltpu.roll(p, 1, 1))
-                    + c[4] * pltpu.roll(p, CX - 1, 1)
+                    (c[0] * p + c[1] * h_rows[far_row, rows, :]) + (c[2] * xr[r + 1, rows, :] + c[3] * pltpu.roll(p, 1, 1))
+                    + (c[4] * pltpu.roll(p, CX - 1, 1) + c[6] * pltpu.roll(merged, (first - 4 * b) % CX, 1))
                 )
                 zr[r_in, rows, :] = zr[r_in, rows, :] + c[5] * p
 
-    add_rows(has_up, above, hu_rows.at[1], hu_rows.at[0], 0, 1)
-    add_rows(has_down, below, hd_rows.at[0], hd_rows.at[1], 7, 6)
+    add_rows(has_up, above, 1, 0, 0, 1, lambda: jnp.where(q1, h_corners[0], pltpu.roll(h_corners[1], CX - 2, 1)), CX - 1)
+    add_rows(has_down, below, 2, 3, 7, 6, lambda: jnp.where(q3, h_corners[2], pltpu.roll(h_corners[3], CX - 2, 1)), 1)
 
     def add_columns(r, carry):
         lines = [jnp.broadcast_to(zc[half, pl.ds(r, 1), :], (8, CX)) for half in range(2)]
@@ -313,9 +314,9 @@
         column = jnp.sum(jnp.where(lane64 == place, zr[row], 0.0), axis=1, keepdims=True)
         column = jnp.broadcast_to(column, (M, CX))
         average = jnp.sum(column, axis=0, keepdims=True) * (1.0 / M)
-        factor = lax.rsqrt(ones + varis[0, 0, j])
+        factor = lax.rsqrt(ones + obs[1, 0, 0, j])
         values = jnp.sum(jnp.where(diag64, column, 0.0), axis=0, keepdims=True)
-        values = jnp.where(iota((1, CX), 1) < M - 1, values, ones + vals[0, 0, j])
+        values = jnp.where(iota((1, CX), 1) < M - 1, values, ones + obs[0, 0, 0, j])
         picked.append(jnp.where(iota((1, CX), 1) < M, (values - average) * factor, 0.0))
     rf[gx] = jnp.concatenate(
         [picked[0] + pltpu.roll(picked[2], M, 1), picked[1] + pltpu.roll(picked[3], M, 1)], axis=0
@@ -354,9 +355,8 @@
     diagonal = jnp.sum(jnp.where(across == along, low, 0.0), axis=0, keepdims=True)
     gram_ref[pl.ds(16, 8), :] = jnp.where(iota((8, CX), 0) == 0, diagonal, 0.0)
 
-    sent(up_rows, down_rows)
-    sent(up_flow, down_flow, side_flow)
-    sent(up_corners, down_corners, side_halos)
+    for index, group in enumerate(groups):
+        settle(halo_send.at[index], *group)
     wait_all(rf, ngx - 1, gx_send)
 
 
@@ -502,9 +502,8 @@
         res = jnp.dot(left, right, preferred_element_type=F32)
         for half in range(2):
             rows_out[r + half] = res[:, half * CX:(half + 1) * CX] + mean_ref[r + half:r + half + 1, :]
-            pltpu.make_async_copy(rows_out.at[r + half], out_hbm.at[:, r + half, :], out_sem.at[r + half]).start()
-    for r in range(CY):
-        pltpu.make_async_copy(rows_out.at[r], out_hbm.at[:, r, :], out_sem.at[r]).wait()
+            pltpu.make_async_copy(rows_out.at[r + half], out_hbm.at[:, r + half, :], out_sem).start()
+    pltpu.make_async_copy(rows_out, rows_out, out_sem).wait()
 
 
 def near(array):
@@ -532,19 +531,17 @@
             pltpu.VMEM((3, CY, CX), F32),
             pltpu.VMEM((5, CY, CX), F32),
             pltpu.SMEM((1, 1, 4), jnp.int32),
-            pltpu.SMEM((1, 1, 4), F32),
-            pltpu.SMEM((1, 1, 4), F32),
+            pltpu.SMEM((2, 1, 1, 4), F32),
             pltpu.VMEM((16, CX), F32),
             pltpu.VMEM((2, 8, CX), F32),
-            pltpu.VMEM((2, M, CX), F32),
-            pltpu.VMEM((2, M, CX), F32),
-            pltpu.VMEM((16, CX), F32),
-            pltpu.VMEM((16, CX), F32),
-            pltpu.VMEM((4, 16, CX), F32),
+            pltpu.VMEM((8, CX), F32),
+            pltpu.VMEM((4, M, CX), F32),
+            pltpu.VMEM((2, 16, CX), F32),
+            pltpu.VMEM((4, 8, CX), F32),
             pltpu.VMEM((4, 8, CX), F32),
             pltpu.VMEM((2, 8, CX), F32),
             pltpu.VMEM((ngx, 2, CX), F32),
-            dma((13,)), dma((8,)), dma((8,)), dma((4,)), dma((4,)), dma, dma,
+            dma((6,)), dma((4,)), dma((4,)), dma, dma,
         ],
         compiler_params=pltpu.CompilerParams(collective_id=0, has_side_effects=True),
         name="forecast",
@@ -567,7 +564,7 @@
         out_shape=jax.ShapeDtypeStruct((M, CY, CX), F32),
         in_specs=[vmem] * 3,
         out_specs=hbm,
-        scratch_shapes=[pltpu.VMEM((CY, M, CX), F32), dma((CY,))],
+        scratch_shapes=[pltpu.VMEM((CY, M, CX), F32), dma],
         name="analysis",
     )(near(gram), near(hilo), near(mean))
 

time: 39.9 us -> 39 us (0.977)
  Pallas kernels: 39.7 us -> 38.7 us
    pallas_call x1, Pallas kernels: 17.2 us -> 16.5 us  [body(): pl.pallas_call(functools.partial(sum_kernel, ngy), out_shape=pltpu.VMEM((...]
where the time goes in v7:
time: 39 us; the launch traced here: 38.8 us
  Pallas kernels  38.7 us (99%)
    pallas_call x1, Pallas kernels, body(): pl.pallas_call(functools.partial(forecast_kernel, ngy, ngx), out_shape=(p...  18.8 us
    pallas_call x1, Pallas kernels, body(): pl.pallas_call(functools.partial(sum_kernel, ngy), out_shape=pltpu.VMEM((...  16.5 us
    pallas_call x1, Pallas kernels, body(): pl.pallas_call(analysis_kernel, out_shape=jax.ShapeDtypeStruct((M, CY, CX...  3.44 us

profile of v7, /device:TPU:1, one launch (start us, length us, event | category | flops | bytes accessed | tf_op | source)
XLA Modules:
  0.0 38.8 jit_solution(8129551128419418749)
XLA Ops:
  0.0 18.8 %forecast.1 = (f32[24,128]{1,0:T(8,128)S(1)}, bf16[128,1024]{1,0:T(8,128)(2,1)S(1)}, f32[8,128]{1,0:T(8,128)S(1)}) custom-call(f32[64,8,128]{2,1,0:T(8,128)} %x_hbm.1, f32[3,8,128]{2,1,0:T(8,128)} %flow_hbm.1, s32[1,1,4]{2,1,0:T(1,128)} %cell_hbm.1, f32[1,1,4]{2,1,0:T(1,128)} %val_hbm.1, f32[1,1,4]{2,1,0:T(1,128)} %var_hbm.1), custom_call_target="tpu_custom_call" | custom-call | tf_op jit(solution)/shard_map/forecast/pallas_call | solution.py:517
  18.8 16.5 %sums.1.gram_ref = f32[24,128]{1,0:T(8,128)S(1)} custom-call(f32[24,128]{1,0:T(8,128)S(1)} %get-tuple-element.8.part_ref), custom_call_target="tpu_custom_call" | custom-call | tf_op jit(solution)/shard_map/sums/pallas_call | solution.py:549
  35.3 3.4 %analysis.1 = f32[64,8,128]{2,1,0:T(8,128)} custom-call(f32[24,128]{1,0:T(8,128)S(1)} %sums.1.gram_ref, bf16[128,1024]{1,0:T(8,128)(2,1)S(1)} %get-tuple-element.9.hilo_ref, f32[8,128]{1,0:T(8,128)S(1)} %get-tuple-element.10.mean_ref), custom_call_target="tpu_custom_call" | custom-call | tf_op jit(solution)/shard_map/analysis/pallas_call | solution.py:562

commit v8 on v7

--- a/solution.py
+++ b/solution.py
@@ -294,15 +294,12 @@
     add_rows(has_up, above, 1, 0, 0, 1, lambda: jnp.where(q1, h_corners[0], pltpu.roll(h_corners[1], CX - 2, 1)), CX - 1)
     add_rows(has_down, below, 2, 3, 7, 6, lambda: jnp.where(q3, h_corners[2], pltpu.roll(h_corners[3], CX - 2, 1)), 1)
 
-    def add_columns(r, carry):
-        lines = [jnp.broadcast_to(zc[half, pl.ds(r, 1), :], (8, CX)) for half in range(2)]
-        for b in range(8):
-            rows = pl.ds(8 * b, 8)
-            spread = pltpu.roll(lines[b // 4], 32 * (b % 4), 1, stride=4, stride_axis=0)
-            zr[r, rows, :] = zr[r, rows, :] + jnp.where(edge, spread, 0.0)
-        return carry
-
-    lax.fori_loop(0, CY, add_columns, 0)
+    def with_columns(r, b, lines):
+        spread = pltpu.roll(lines[b // 4], 32 * (b % 4), 1, stride=4, stride_axis=0)
+        return zr[r, 8 * b:8 * b + 8, :] + jnp.where(edge, spread, 0.0)
+
+    def column_lines(r):
+        return [jnp.broadcast_to(zc[half, pl.ds(r, 1), :], (8, CX)) for half in range(2)]
 
     lane64 = iota((M, CX), 1)
     diag64 = lane64 == iota((M, CX), 0)
@@ -311,7 +308,9 @@
     for j in range(4):
         cell = cells[0, 0, j]
         row, place = lax.shift_right_logical(cell, 7), cell & (CX - 1)
-        column = jnp.sum(jnp.where(lane64 == place, zr[row], 0.0), axis=1, keepdims=True)
+        lines = column_lines(row)
+        field = jnp.concatenate([with_columns(row, b, lines) for b in range(8)], axis=0)
+        column = jnp.sum(jnp.where(lane64 == place, field, 0.0), axis=1, keepdims=True)
         column = jnp.broadcast_to(column, (M, CX))
         average = jnp.sum(column, axis=0, keepdims=True) * (1.0 / M)
         factor = lax.rsqrt(ones + obs[1, 0, 0, j])
@@ -333,7 +332,8 @@
         copy.start()
 
     for r in range(CY):
-        field = zr[r]
+        lines = column_lines(r)
+        field = jnp.concatenate([with_columns(r, b, lines) for b in range(8)], axis=0)
         mean = jnp.sum(field, axis=0, keepdims=True) * (1.0 / M)
         mean_ref[pl.ds(r, 1), :] = mean
         field = field - mean

time: 39 us -> 38.6 us (0.990)
  Pallas kernels: 38.7 us -> 38.3 us
    pallas_call x1, Pallas kernels: 18.8 us -> 18.4 us  [body(): pl.pallas_call(functools.partial(forecast_kernel, ngy, ngx), out_shape=(p...]
where the time goes in v8:
time: 38.6 us; the launch traced here: 38.3 us
  Pallas kernels  38.3 us (99%)
    pallas_call x1, Pallas kernels, body(): pl.pallas_call(functools.partial(forecast_kernel, ngy, ngx), out_shape=(p...  18.4 us
    pallas_call x1, Pallas kernels, body(): pl.pallas_call(functools.partial(sum_kernel, ngy), out_shape=pltpu.VMEM((...  16.5 us
    pallas_call x1, Pallas kernels, body(): pl.pallas_call(analysis_kernel, out_shape=jax.ShapeDtypeStruct((M, CY, CX...  3.44 us

profile of v8, /device:TPU:1, one launch (start us, length us, event | category | flops | bytes accessed | tf_op | source)
XLA Modules:
  0.0 38.3 jit_solution(17392426341591062642)
XLA Ops:
  0.0 18.4 %forecast.1 = (f32[24,128]{1,0:T(8,128)S(1)}, bf16[128,1024]{1,0:T(8,128)(2,1)S(1)}, f32[8,128]{1,0:T(8,128)S(1)}) custom-call(f32[64,8,128]{2,1,0:T(8,128)} %x_hbm.1, f32[3,8,128]{2,1,0:T(8,128)} %flow_hbm.1, s32[1,1,4]{2,1,0:T(1,128)} %cell_hbm.1, f32[1,1,4]{2,1,0:T(1,128)} %val_hbm.1, f32[1,1,4]{2,1,0:T(1,128)} %var_hbm.1), custom_call_target="tpu_custom_call" | custom-call | tf_op jit(solution)/shard_map/forecast/pallas_call | solution.py:517
  18.4 16.5 %sums.1.gram_ref = f32[24,128]{1,0:T(8,128)S(1)} custom-call(f32[24,128]{1,0:T(8,128)S(1)} %get-tuple-element.8.part_ref), custom_call_target="tpu_custom_call" | custom-call | tf_op jit(solution)/shard_map/sums/pallas_call | solution.py:549
  34.9 3.4 %analysis.1 = f32[64,8,128]{2,1,0:T(8,128)} custom-call(f32[24,128]{1,0:T(8,128)S(1)} %sums.1.gram_ref, bf16[128,1024]{1,0:T(8,128)(2,1)S(1)} %get-tuple-element.9.hilo_ref, f32[8,128]{1,0:T(8,128)S(1)} %get-tuple-element.10.mean_ref), custom_call_target="tpu_custom_call" | custom-call | tf_op jit(solution)/shard_map/analysis/pallas_call | solution.py:562

commit v9 on v8

--- a/solution.py
+++ b/solution.py
@@ -30,7 +30,7 @@
     x_hbm, flow_hbm, cell_hbm, val_hbm, var_hbm,
     gram_ref, hilo_ref, mean_ref,
     xb, xr, yr, zr, fl, cf, cells, obs, qs, fs, ct, h_rows, h_sides, h_corners, fh, zc, rf,
-    load_sem, halo_send, halo_recv, gx_send, gx_recv,
+    load_sem, corner_send, halo_recv, gx_recv,
 ):
     gy = lax.axis_index("gy")
     gx = lax.axis_index("gx")
@@ -79,9 +79,12 @@
     q0, q1, q3 = quad == 0, quad == 1, quad == 3
     west_side = quad >= 2
 
+    sends = [load_sem.at[0], load_sem.at[2], load_sem.at[1], corner_send]
+    gx_send = load_sem.at[3]
+
     def remote(src, dst, index, target):
         return pltpu.make_async_remote_copy(
-            src_ref=src, dst_ref=dst, send_sem=halo_send.at[index], recv_sem=halo_recv.at[index],
+            src_ref=src, dst_ref=dst, send_sem=sends[index], recv_sem=halo_recv.at[index],
             device_id=target, device_id_type=MESH,
         )
 
@@ -128,16 +131,6 @@
         fs[0, pl.ds(3 + i, 1), :] = fl[i, 7:8, :]
     loaded(xr.at[pl.ds(0, 4)], 1)
 
-    @pl.when(both)
-    def _():
-        pl.semaphore_wait(barrier, ngx + 5)
-
-    @pl.when(jnp.logical_not(both))
-    def _():
-        pl.semaphore_wait(barrier, ngx + 2)
-
-    start(2, [(xr.at[pl.ds(1, 2)], h_rows.at[pl.ds(2, 2)], gx)], [(xr.at[pl.ds(7, 2)], h_rows.at[pl.ds(0, 2)], gx)])
-    start(0, [(fs.at[0], fh.at[1], gx)], [(fs.at[0], fh.at[0], gx)], (fs.at[1], fh.at[2]), (fs.at[1], fh.at[3]))
     ends = l0 | l127
     tile = jnp.zeros((8, CX), F32)
     for b in range(8):
@@ -145,20 +138,30 @@
         tile = tile + pltpu.roll(jnp.where(ends, xr[1, rows, :], 0.0), 4 * b, 1)
         tile = tile + pltpu.roll(jnp.where(ends, xr[8, rows, :], 0.0), 4 * b + 2, 1)
     ct[...] = tile
+
+    @pl.when(both)
+    def _():
+        pl.semaphore_wait(barrier, ngx + 5)
+
+    @pl.when(jnp.logical_not(both))
+    def _():
+        pl.semaphore_wait(barrier, ngx + 2)
+
     start(
         3,
         [(ct, h_corners.at[3], left), (ct, h_corners.at[2], right)],
         [(ct, h_corners.at[1], left), (ct, h_corners.at[0], right)],
     )
+    start(0, [(fs.at[0], fh.at[1], gx)], [(fs.at[0], fh.at[0], gx)], (fs.at[1], fh.at[2]), (fs.at[1], fh.at[3]))
+    start(2, [(xr.at[pl.ds(1, 2)], h_rows.at[pl.ds(2, 2)], gx)], [(xr.at[pl.ds(7, 2)], h_rows.at[pl.ds(0, 2)], gx)])
     loaded(xb, 2)
 
     def pack(half):
-        def body(i, q):
-            for j in range(8):
-                m = i * 8 + j
-                q = q + pltpu.roll(jnp.where(edge, xb[half * 32 + m], 0.0), lax.rem(CX - 4 * m, CX), 1)
-            return q
-        return lax.fori_loop(0, 4, body, jnp.zeros((8, CX), F32))
+        sums = [None] * 4
+        for m in range(32):
+            piece = pltpu.roll(jnp.where(edge, xb[half * 32 + m], 0.0), (CX - 4 * m) % CX, 1)
+            sums[m % 4] = piece if m < 4 else sums[m % 4] + piece
+        return (sums[0] + sums[1]) + (sums[2] + sums[3])
 
     qa, qb = pack(0), pack(1)
     qs[pl.ds(0, 8), :] = qa
@@ -341,13 +344,16 @@
         hilo_ref[pl.ds(0, M), pl.ds(r * CX, CX)] = high
         hilo_ref[pl.ds(M, M), pl.ds(r * CX, CX)] = (field - high.astype(F32)).astype(BF16)
 
+    for index, group in enumerate(groups):
+        settle(sends[index], *group)
+
     wait_all(rf, ngx - 1, gx_recv)
     gathered = jnp.concatenate([rf[i] for i in range(ngx)], axis=0)
     lane32 = iota((2 * ngx, CX), 1)
     rows = jnp.concatenate(
         [jnp.where(lane32 < M, gathered, 0.0), jnp.where(lane32 < M, pltpu.roll(gathered, M, 1), 0.0)], axis=0
     )
-    gram = jnp.dot(rows.T, rows, precision=lax.Precision.HIGHEST, preferred_element_type=F32)
+    gram = jnp.dot(rows.T[0:M], rows, precision=lax.Precision.HIGHEST, preferred_element_type=F32)
     high, low = gram[0:32], pltpu.roll(gram[32:64], CX - 32, 1)
     across, along = iota((32, CX), 1), iota((32, CX), 0)
     square = jnp.where((across < 32) & (across > along), low, high)
@@ -355,8 +361,6 @@
     diagonal = jnp.sum(jnp.where(across == along, low, 0.0), axis=0, keepdims=True)
     gram_ref[pl.ds(16, 8), :] = jnp.where(iota((8, CX), 0) == 0, diagonal, 0.0)
 
-    for index, group in enumerate(groups):
-        settle(halo_send.at[index], *group)
     wait_all(rf, ngx - 1, gx_send)
 
 
@@ -541,7 +545,7 @@
             pltpu.VMEM((4, 8, CX), F32),
             pltpu.VMEM((2, 8, CX), F32),
             pltpu.VMEM((ngx, 2, CX), F32),
-            dma((6,)), dma((4,)), dma((4,)), dma, dma,
+            dma((6,)), dma, dma((4,)), dma,
         ],
         compiler_params=pltpu.CompilerParams(collective_id=0, has_side_effects=True),
         name="forecast",

time: 38.6 us -> 38.4 us (level)
    pallas_call x1, Pallas kernels: 18.4 us -> 17.7 us  [body(): pl.pallas_call(functools.partial(forecast_kernel, ngy, ngx), out_shape=(p...]
    pallas_call x1, Pallas kernels: 16.5 us -> 17 us  [body(): pl.pallas_call(functools.partial(sum_kernel, ngy), out_shape=pltpu.VMEM((...]
where the time goes in v9:
time: 38.4 us; the launch traced here: 38.1 us
  Pallas kernels  38.1 us (99%)
    pallas_call x1, Pallas kernels, body(): pl.pallas_call(functools.partial(forecast_kernel, ngy, ngx), out_shape=(p...  17.7 us
    pallas_call x1, Pallas kernels, body(): pl.pallas_call(functools.partial(sum_kernel, ngy), out_shape=pltpu.VMEM((...  17 us
    pallas_call x1, Pallas kernels, body(): pl.pallas_call(analysis_kernel, out_shape=jax.ShapeDtypeStruct((M, CY, CX...  3.44 us

profile of v9, /device:TPU:1, one launch (start us, length us, event | category | flops | bytes accessed | tf_op | source)
XLA Modules:
  0.0 38.1 jit_solution(17973159288337167582)
XLA Ops:
  0.0 17.7 %forecast.1 = (f32[24,128]{1,0:T(8,128)S(1)}, bf16[128,1024]{1,0:T(8,128)(2,1)S(1)}, f32[8,128]{1,0:T(8,128)S(1)}) custom-call(f32[64,8,128]{2,1,0:T(8,128)} %x_hbm.1, f32[3,8,128]{2,1,0:T(8,128)} %flow_hbm.1, s32[1,1,4]{2,1,0:T(1,128)} %cell_hbm.1, f32[1,1,4]{2,1,0:T(1,128)} %val_hbm.1, f32[1,1,4]{2,1,0:T(1,128)} %var_hbm.1), custom_call_target="tpu_custom_call" | custom-call | tf_op jit(solution)/shard_map/forecast/pallas_call | solution.py:521
  17.7 17.0 %sums.1.gram_ref = f32[24,128]{1,0:T(8,128)S(1)} custom-call(f32[24,128]{1,0:T(8,128)S(1)} %get-tuple-element.8.part_ref), custom_call_target="tpu_custom_call" | custom-call | tf_op jit(solution)/shard_map/sums/pallas_call | solution.py:553
  34.7 3.4 %analysis.1 = f32[64,8,128]{2,1,0:T(8,128)} custom-call(f32[24,128]{1,0:T(8,128)S(1)} %sums.1.gram_ref, bf16[128,1024]{1,0:T(8,128)(2,1)S(1)} %get-tuple-element.9.hilo_ref, f32[8,128]{1,0:T(8,128)S(1)} %get-tuple-element.10.mean_ref), custom_call_target="tpu_custom_call" | custom-call | tf_op jit(solution)/shard_map/analysis/pallas_call | solution.py:566

commit v10 on v9

--- a/solution.py
+++ b/solution.py
@@ -445,6 +445,8 @@
     ]
 
     lower = [None] * 8
+    heads = []
+    target_high = pltpu.roll(jnp.broadcast_to(target_row, (8, CX)), M, 1)
     nothing = 0.0 * packed[0:8]
     for p in range(16):
         b, o = p // 2, 4 * (p % 2)
@@ -459,23 +461,24 @@
 
         det = d[0, 0] * d[1, 1] - d[1, 0] * d[1, 0]
         inv = 1.0 / det
+        f00 = d[1, 1] * d[2, 0] - d[1, 0] * d[2, 1]
+        f10 = d[0, 0] * d[2, 1] - d[1, 0] * d[2, 0]
+        f01 = d[1, 1] * d[3, 0] - d[1, 0] * d[3, 1]
+        f11 = d[0, 0] * d[3, 1] - d[1, 0] * d[3, 0]
+        g00 = det * d[2, 2] - (d[2, 0] * f00 + d[2, 1] * f10)
+        g10 = det * d[3, 2] - (d[3, 0] * f00 + d[3, 1] * f10)
+        g11 = det * d[3, 3] - (d[3, 0] * f01 + d[3, 1] * f11)
+        det2 = g00 * g11 - g10 * g10
         i00, i10, i11 = d[1, 1] * inv, -d[1, 0] * inv, d[0, 0] * inv
-        e00 = i00 * d[2, 0] + i10 * d[2, 1]
-        e10 = i10 * d[2, 0] + i11 * d[2, 1]
-        e01 = i00 * d[3, 0] + i10 * d[3, 1]
-        e11 = i10 * d[3, 0] + i11 * d[3, 1]
-        c00 = d[2, 2] - (d[2, 0] * e00 + d[2, 1] * e10)
-        c10 = d[3, 2] - (d[3, 0] * e00 + d[3, 1] * e10)
-        c11 = d[3, 3] - (d[3, 0] * e01 + d[3, 1] * e11)
+        e00, e10, e01, e11 = f00 * inv, f10 * inv, f01 * inv, f11 * inv
         r2 = r[2] - (e00 * r[0] + e10 * r[1])
         r3 = r[3] - (e01 * r[0] + e11 * r[1])
-        det2 = c00 * c11 - c10 * c10
         if p < 15:
             u0 = i00 * r[0] + i10 * r[1]
             u1 = i10 * r[0] + i11 * r[1]
-            inv2 = 1.0 / det2
-            z2 = (c11 * r2 - c10 * r3) * inv2
-            z3 = (c00 * r3 - c10 * r2) * inv2
+            inv2 = det * (1.0 / det2)
+            z2 = (g11 * r2 - g10 * r3) * inv2
+            z3 = (g00 * r3 - g10 * r2) * inv2
             z0 = u0 - (e00 * z2 + e01 * z3)
             z1 = u1 - (e10 * z2 + e11 * z3)
             z = (z0, z1, z2, z3)
@@ -485,19 +488,20 @@
                 a[i] = jnp.where(sub >= 4, new, a[i]) if i == b else new
         n0 = r[0] * lax.rsqrt(d[0, 0])
         n1 = (d[0, 0] * r[1] - d[1, 0] * r[0]) * lax.rsqrt(d[0, 0] * det)
+        c00, c10 = g00 * inv, g10 * inv
         n2 = r2 * lax.rsqrt(c00)
-        n3 = (c00 * r3 - c10 * r2) * lax.rsqrt(c00 * det2)
+        n3 = (c00 * r3 - c10 * r2) * lax.rsqrt(c00 * (det2 * inv * inv))
         rows = jnp.where(sub == o, n0, jnp.where(sub == o + 1, n1, jnp.where(sub == o + 2, n2, n3)))
         lower[b] = rows if o == 0 else jnp.where(sub >= 4, rows, lower[b])
-    lower = [pltpu.roll(jnp.where(lane >= M, v, 0.0), M, 1) for v in lower]
-    heads = [jnp.sum(v * target_row, axis=1, keepdims=True) for v in lower]
+        if o:
+            lower[b] = jnp.where(lane >= M, lower[b], 0.0)
+            heads.append(jnp.sum(lower[b] * target_high, axis=1, keepdims=True))
     weight = jnp.sum(functools.reduce(jnp.add, [v * h for v, h in zip(lower, heads)]), axis=0, keepdims=True)
     root = math.sqrt(M - 1.0)
     mix = jnp.concatenate([root * v + weight for v in lower], axis=0)
-    high = mix.astype(BF16).astype(F32)
-    low = mix - high
-    pair = jnp.where(iota((M, CX), 1) < M, high, pltpu.roll(high, M, 1)).astype(BF16)
-    low_pair = jnp.where(iota((M, CX), 1) < M, low, pltpu.roll(low, M, 1)).astype(BF16)
+    mix = jnp.where(iota((M, CX), 1) < M, pltpu.roll(mix, M, 1), mix)
+    high = mix.astype(BF16)
+    pair, low_pair = high, (mix - high.astype(F32)).astype(BF16)
     left = jnp.concatenate([pair, low_pair], axis=1)
     for r in range(0, CY, 2):
         cols = pl.ds(r * CX, 2 * CX)

time: 38.4 us -> 38.2 us (level)
  no operation moved by 1% of the time
where the time goes in v10:
time: 38.2 us; the launch traced here: 37.9 us
  Pallas kernels  37.9 us (99%)
    pallas_call x1, Pallas kernels, body(): pl.pallas_call(functools.partial(forecast_kernel, ngy, ngx), out_shape=(p...  17.7 us
    pallas_call x1, Pallas kernels, body(): pl.pallas_call(functools.partial(sum_kernel, ngy), out_shape=pltpu.VMEM((...  17 us
    pallas_call x1, Pallas kernels, body(): pl.pallas_call(analysis_kernel, out_shape=jax.ShapeDtypeStruct((M, CY, CX...  3.25 us

profile of v10, /device:TPU:1, one launch (start us, length us, event | category | flops | bytes accessed | tf_op | source)
XLA Modules:
  0.0 37.9 jit_solution(9826464994475004229)
XLA Ops:
  0.0 17.7 %forecast.1 = (f32[24,128]{1,0:T(8,128)S(1)}, bf16[128,1024]{1,0:T(8,128)(2,1)S(1)}, f32[8,128]{1,0:T(8,128)S(1)}) custom-call(f32[64,8,128]{2,1,0:T(8,128)} %x_hbm.1, f32[3,8,128]{2,1,0:T(8,128)} %flow_hbm.1, s32[1,1,4]{2,1,0:T(1,128)} %cell_hbm.1, f32[1,1,4]{2,1,0:T(1,128)} %val_hbm.1, f32[1,1,4]{2,1,0:T(1,128)} %var_hbm.1), custom_call_target="tpu_custom_call" | custom-call | tf_op jit(solution)/shard_map/forecast/pallas_call | solution.py:525
  17.7 17.0 %sums.1.gram_ref = f32[24,128]{1,0:T(8,128)S(1)} custom-call(f32[24,128]{1,0:T(8,128)S(1)} %get-tuple-element.8.part_ref), custom_call_target="tpu_custom_call" | custom-call | tf_op jit(solution)/shard_map/sums/pallas_call | solution.py:557
  34.7 3.2 %analysis.1 = f32[64,8,128]{2,1,0:T(8,128)} custom-call(f32[24,128]{1,0:T(8,128)S(1)} %sums.1.gram_ref, bf16[128,1024]{1,0:T(8,128)(2,1)S(1)} %get-tuple-element.9.hilo_ref, f32[8,128]{1,0:T(8,128)S(1)} %get-tuple-element.10.mean_ref), custom_call_target="tpu_custom_call" | custom-call | tf_op jit(solution)/shard_map/analysis/pallas_call | solution.py:570

commit v11 on v10

--- a/solution.py
+++ b/solution.py
@@ -375,7 +375,7 @@
     nz = ngy // NX4
     zpos = gy // NX4
     xpos = lax.rem(gy, NX4)
-    z_partners = [(lax.rem(gy + NX4 * i, ngy), gx) for i in range(1, nz)]
+    z_partners = [(lax.rem(gy + NX4 * i, ngy), gx) for i in sorted(range(1, nz), key=lambda i: -min(i, nz - i))]
     x_partners = [(zpos * NX4 + lax.rem(xpos + i, NX4), gx) for i in (2, 1, 3)]
     barrier = pltpu.get_barrier_semaphore()
     for partner in z_partners + x_partners:
@@ -477,14 +477,18 @@
             u0 = i00 * r[0] + i10 * r[1]
             u1 = i10 * r[0] + i11 * r[1]
             inv2 = det * (1.0 / det2)
-            z2 = (g11 * r2 - g10 * r3) * inv2
-            z3 = (g00 * r3 - g10 * r2) * inv2
+            t2, t3 = g11 * r2 - g10 * r3, g00 * r3 - g10 * r2
+            z2, z3 = t2 * inv2, t3 * inv2
             z0 = u0 - (e00 * z2 + e01 * z3)
             z1 = u1 - (e10 * z2 + e11 * z3)
             z = (z0, z1, z2, z3)
             for i in range(b if o == 0 else b + 1, 8):
-                update = (cols[0, i] * z[0] + cols[1, i] * z[1]) + (cols[2, i] * z[2] + cols[3, i] * z[3])
-                new = a[i] - update
+                if i == (b if o == 0 else b + 1):
+                    m2 = cols[2, i] - (cols[0, i] * e00 + cols[1, i] * e10)
+                    m3 = cols[3, i] - (cols[0, i] * e01 + cols[1, i] * e11)
+                    new = (a[i] - (cols[0, i] * u0 + cols[1, i] * u1)) - inv2 * (m2 * t2 + m3 * t3)
+                else:
+                    new = a[i] - ((cols[0, i] * z[0] + cols[1, i] * z[1]) + (cols[2, i] * z[2] + cols[3, i] * z[3]))
                 a[i] = jnp.where(sub >= 4, new, a[i]) if i == b else new
         n0 = r[0] * lax.rsqrt(d[0, 0])
         n1 = (d[0, 0] * r[1] - d[1, 0] * r[0]) * lax.rsqrt(d[0, 0] * det)

time: 38.2 us -> 38 us (level)
  no operation moved by 1% of the time
where the time goes in v11:
time: 38 us; the launch traced here: 37.8 us
  Pallas kernels  37.7 us (99%)
    pallas_call x1, Pallas kernels, body(): pl.pallas_call(functools.partial(forecast_kernel, ngy, ngx), out_shape=(p...  17.7 us
    pallas_call x1, Pallas kernels, body(): pl.pallas_call(functools.partial(sum_kernel, ngy), out_shape=pltpu.VMEM((...  17 us
    pallas_call x1, Pallas kernels, body(): pl.pallas_call(analysis_kernel, out_shape=jax.ShapeDtypeStruct((M, CY, CX...  3.09 us

profile of v11, /device:TPU:1, one launch (start us, length us, event | category | flops | bytes accessed | tf_op | source)
XLA Modules:
  0.0 37.8 jit_solution(858076647327614771)
XLA Ops:
  0.0 17.7 %forecast.1 = (f32[24,128]{1,0:T(8,128)S(1)}, bf16[128,1024]{1,0:T(8,128)(2,1)S(1)}, f32[8,128]{1,0:T(8,128)S(1)}) custom-call(f32[64,8,128]{2,1,0:T(8,128)} %x_hbm.1, f32[3,8,128]{2,1,0:T(8,128)} %flow_hbm.1, s32[1,1,4]{2,1,0:T(1,128)} %cell_hbm.1, f32[1,1,4]{2,1,0:T(1,128)} %val_hbm.1, f32[1,1,4]{2,1,0:T(1,128)} %var_hbm.1), custom_call_target="tpu_custom_call" | custom-call | tf_op jit(solution)/shard_map/forecast/pallas_call | solution.py:529
  17.7 17.0 %sums.1.gram_ref = f32[24,128]{1,0:T(8,128)S(1)} custom-call(f32[24,128]{1,0:T(8,128)S(1)} %get-tuple-element.8.part_ref), custom_call_target="tpu_custom_call" | custom-call | tf_op jit(solution)/shard_map/sums/pallas_call | solution.py:561
  34.7 3.1 %analysis.1 = f32[64,8,128]{2,1,0:T(8,128)} custom-call(f32[24,128]{1,0:T(8,128)S(1)} %sums.1.gram_ref, bf16[128,1024]{1,0:T(8,128)(2,1)S(1)} %get-tuple-element.9.hilo_ref, f32[8,128]{1,0:T(8,128)S(1)} %get-tuple-element.10.mean_ref), custom_call_target="tpu_custom_call" | custom-call | tf_op jit(solution)/shard_map/analysis/pallas_call | solution.py:574

commit v12 on v11

--- a/solution.py
+++ b/solution.py
@@ -380,27 +380,27 @@
     barrier = pltpu.get_barrier_semaphore()
     for partner in z_partners + x_partners:
         pl.semaphore_signal(barrier, inc=1, device_id=partner, device_id_type=MESH)
-    rz[zpos] = part_ref[...]
     pl.semaphore_wait(barrier, nz + NX4 - 2)
 
     def wait_rows(buffer, count, sem):
         piece = buffer.at[pl.ds(0, count), pl.ds(0, 17)]
         pltpu.make_async_copy(piece, piece, sem).wait()
 
-    def spread(buffer, slot, partners, send, recv):
+    def spread(source, buffer, slot, partners, send, recv):
         for partner in partners:
             pltpu.make_async_remote_copy(
-                src_ref=buffer.at[slot, pl.ds(0, 17)], dst_ref=buffer.at[slot, pl.ds(0, 17)], send_sem=send, recv_sem=recv,
+                src_ref=source.at[pl.ds(0, 17)], dst_ref=buffer.at[slot, pl.ds(0, 17)], send_sem=send, recv_sem=recv,
                 device_id=partner, device_id_type=MESH,
             ).start()
 
-    spread(rz, zpos, z_partners, z_send, z_recv)
+    spread(part_ref, rz, zpos, z_partners, z_send, z_recv)
+    rz[zpos] = part_ref[...]
     wait_rows(rz, nz - 1, z_recv)
     part = rz[0]
     for i in range(1, nz):
         part = part + rz[i]
     rx[xpos] = part
-    spread(rx, xpos, x_partners, x_send, x_recv)
+    spread(rx.at[xpos], rx, xpos, x_partners, x_send, x_recv)
     wait_rows(rx, NX4 - 1, x_recv)
     gram_ref[...] = (rx[0] + rx[1]) + (rx[2] + rx[3])
     wait_rows(rz, nz - 1, z_send)

time: 38 us -> 38 us (level)
  no operation moved by 1% of the time
where the time goes in v12:
time: 38 us; the launch traced here: 37.8 us
  Pallas kernels  37.7 us (99%)
    pallas_call x1, Pallas kernels, body(): pl.pallas_call(functools.partial(forecast_kernel, ngy, ngx), out_shape=(p...  17.7 us
    pallas_call x1, Pallas kernels, body(): pl.pallas_call(functools.partial(sum_kernel, ngy), out_shape=pltpu.VMEM((...  17 us
    pallas_call x1, Pallas kernels, body(): pl.pallas_call(analysis_kernel, out_shape=jax.ShapeDtypeStruct((M, CY, CX...  3.09 us

profile of v12, /device:TPU:1, one launch (start us, length us, event | category | flops | bytes accessed | tf_op | source)
XLA Modules:
  0.0 37.8 jit_solution(1365134437912937081)
XLA Ops:
  0.0 17.7 %forecast.1 = (f32[24,128]{1,0:T(8,128)S(1)}, bf16[128,1024]{1,0:T(8,128)(2,1)S(1)}, f32[8,128]{1,0:T(8,128)S(1)}) custom-call(f32[64,8,128]{2,1,0:T(8,128)} %x_hbm.1, f32[3,8,128]{2,1,0:T(8,128)} %flow_hbm.1, s32[1,1,4]{2,1,0:T(1,128)} %cell_hbm.1, f32[1,1,4]{2,1,0:T(1,128)} %val_hbm.1, f32[1,1,4]{2,1,0:T(1,128)} %var_hbm.1), custom_call_target="tpu_custom_call" | custom-call | tf_op jit(solution)/shard_map/forecast/pallas_call | solution.py:529
  17.7 17.0 %sums.1.gram_ref = f32[24,128]{1,0:T(8,128)S(1)} custom-call(f32[24,128]{1,0:T(8,128)S(1)} %get-tuple-element.8.part_ref), custom_call_target="tpu_custom_call" | custom-call | tf_op jit(solution)/shard_map/sums/pallas_call | solution.py:561
  34.7 3.1 %analysis.1 = f32[64,8,128]{2,1,0:T(8,128)} custom-call(f32[24,128]{1,0:T(8,128)S(1)} %sums.1.gram_ref, bf16[128,1024]{1,0:T(8,128)(2,1)S(1)} %get-tuple-element.9.hilo_ref, f32[8,128]{1,0:T(8,128)S(1)} %get-tuple-element.10.mean_ref), custom_call_target="tpu_custom_call" | custom-call | tf_op jit(solution)/shard_map/analysis/pallas_call | solution.py:574

commit v13 on v12

--- a/solution.py
+++ b/solution.py
@@ -347,6 +347,7 @@
     for index, group in enumerate(groups):
         settle(sends[index], *group)
 
+    wait_all(rf, ngx - 1, gx_send)
     wait_all(rf, ngx - 1, gx_recv)
     gathered = jnp.concatenate([rf[i] for i in range(ngx)], axis=0)
     lane32 = iota((2 * ngx, CX), 1)
@@ -361,8 +362,6 @@
     diagonal = jnp.sum(jnp.where(across == along, low, 0.0), axis=0, keepdims=True)
     gram_ref[pl.ds(16, 8), :] = jnp.where(iota((8, CX), 0) == 0, diagonal, 0.0)
 
-    wait_all(rf, ngx - 1, gx_send)
-
 
 def wait_all(buffer, count, sem):
     piece = buffer.at[pl.ds(0, count)]
@@ -401,9 +400,9 @@
         part = part + rz[i]
     rx[xpos] = part
     spread(rx.at[xpos], rx, xpos, x_partners, x_send, x_recv)
+    wait_rows(rz, nz - 1, z_send)
     wait_rows(rx, NX4 - 1, x_recv)
     gram_ref[...] = (rx[0] + rx[1]) + (rx[2] + rx[3])
-    wait_rows(rz, nz - 1, z_send)
     wait_rows(rx, NX4 - 1, x_send)
 
 

time: 38 us -> 38 us (level)
  no operation moved by 1% of the time
where the time goes in v13:
time: 38 us; the launch traced here: 37.8 us
  Pallas kernels  37.7 us (99%)
    pallas_call x1, Pallas kernels, body(): pl.pallas_call(functools.partial(forecast_kernel, ngy, ngx), out_shape=(p...  17.7 us
    pallas_call x1, Pallas kernels, body(): pl.pallas_call(functools.partial(sum_kernel, ngy), out_shape=pltpu.VMEM((...  17 us
    pallas_call x1, Pallas kernels, body(): pl.pallas_call(analysis_kernel, out_shape=jax.ShapeDtypeStruct((M, CY, CX...  3.09 us

profile of v13, /device:TPU:1, one launch (start us, length us, event | category | flops | bytes accessed | tf_op | source)
XLA Modules:
  0.0 37.8 jit_solution(3671358123517116113)
XLA Ops:
  0.0 17.7 %forecast.1 = (f32[24,128]{1,0:T(8,128)S(1)}, bf16[128,1024]{1,0:T(8,128)(2,1)S(1)}, f32[8,128]{1,0:T(8,128)S(1)}) custom-call(f32[64,8,128]{2,1,0:T(8,128)} %x_hbm.1, f32[3,8,128]{2,1,0:T(8,128)} %flow_hbm.1, s32[1,1,4]{2,1,0:T(1,128)} %cell_hbm.1, f32[1,1,4]{2,1,0:T(1,128)} %val_hbm.1, f32[1,1,4]{2,1,0:T(1,128)} %var_hbm.1), custom_call_target="tpu_custom_call" | custom-call | tf_op jit(solution)/shard_map/forecast/pallas_call | solution.py:528
  17.7 17.0 %sums.1.gram_ref = f32[24,128]{1,0:T(8,128)S(1)} custom-call(f32[24,128]{1,0:T(8,128)S(1)} %get-tuple-element.8.part_ref), custom_call_target="tpu_custom_call" | custom-call | tf_op jit(solution)/shard_map/sums/pallas_call | solution.py:560
  34.7 3.1 %analysis.1 = f32[64,8,128]{2,1,0:T(8,128)} custom-call(f32[24,128]{1,0:T(8,128)S(1)} %sums.1.gram_ref, bf16[128,1024]{1,0:T(8,128)(2,1)S(1)} %get-tuple-element.9.hilo_ref, f32[8,128]{1,0:T(8,128)S(1)} %get-tuple-element.10.mean_ref), custom_call_target="tpu_custom_call" | custom-call | tf_op jit(solution)/shard_map/analysis/pallas_call | solution.py:573

commit v14 on v13

--- a/solution.py
+++ b/solution.py
@@ -45,9 +45,9 @@
     def loaded(piece, index):
         pltpu.make_async_copy(piece, piece, load_sem.at[index]).wait()
 
-    load(flow_hbm, fl, 0)
     for r in (0, 7, 1, 6):
         load(x_hbm.at[:, r, :], xr.at[r + 1], 1)
+    load(flow_hbm, fl, 0)
     load(x_hbm, xb, 2)
     for r in (2, 3, 4, 5):
         load(x_hbm.at[:, r, :], xr.at[r + 1], 3)

time: 38 us -> 38 us (level)
  no operation moved by 1% of the time
where the time goes in v14:
time: 38 us; the launch traced here: 37.8 us
  Pallas kernels  37.7 us (99%)
    pallas_call x1, Pallas kernels, body(): pl.pallas_call(functools.partial(forecast_kernel, ngy, ngx), out_shape=(p...  17.7 us
    pallas_call x1, Pallas kernels, body(): pl.pallas_call(functools.partial(sum_kernel, ngy), out_shape=pltpu.VMEM((...  17 us
    pallas_call x1, Pallas kernels, body(): pl.pallas_call(analysis_kernel, out_shape=jax.ShapeDtypeStruct((M, CY, CX...  3.09 us

profile of v14, /device:TPU:1, one launch (start us, length us, event | category | flops | bytes accessed | tf_op | source)
XLA Modules:
  0.0 37.8 jit_solution(7381944062338518212)
XLA Ops:
  0.0 17.7 %forecast.1 = (f32[24,128]{1,0:T(8,128)S(1)}, bf16[128,1024]{1,0:T(8,128)(2,1)S(1)}, f32[8,128]{1,0:T(8,128)S(1)}) custom-call(f32[64,8,128]{2,1,0:T(8,128)} %x_hbm.1, f32[3,8,128]{2,1,0:T(8,128)} %flow_hbm.1, s32[1,1,4]{2,1,0:T(1,128)} %cell_hbm.1, f32[1,1,4]{2,1,0:T(1,128)} %val_hbm.1, f32[1,1,4]{2,1,0:T(1,128)} %var_hbm.1), custom_call_target="tpu_custom_call" | custom-call | tf_op jit(solution)/shard_map/forecast/pallas_call | solution.py:528
  17.7 17.0 %sums.1.gram_ref = f32[24,128]{1,0:T(8,128)S(1)} custom-call(f32[24,128]{1,0:T(8,128)S(1)} %get-tuple-element.8.part_ref), custom_call_target="tpu_custom_call" | custom-call | tf_op jit(solution)/shard_map/sums/pallas_call | solution.py:560
  34.7 3.1 %analysis.1 = f32[64,8,128]{2,1,0:T(8,128)} custom-call(f32[24,128]{1,0:T(8,128)S(1)} %sums.1.gram_ref, bf16[128,1024]{1,0:T(8,128)(2,1)S(1)} %get-tuple-element.9.hilo_ref, f32[8,128]{1,0:T(8,128)S(1)} %get-tuple-element.10.mean_ref), custom_call_target="tpu_custom_call" | custom-call | tf_op jit(solution)/shard_map/analysis/pallas_call | solution.py:573
